TPU v7x, 256 devices: a whole 4x4x8 slice. The times are simulated.
256 devices in a mesh: seq: 32 (over z, y), grp: 8 (over x, core).
Axes of the slice: x: 4, y: 4, z: 8, core: 2. Of those that a mesh axis runs over, the one named last changes fastest.
Arguments:
- x_in: bfloat16 [4096, 8192], P('seq', 'grp'), may hold values from -6 to 6
- multiplier_channels: bfloat16 [4096, 8192], P('seq', 'grp'), may hold values from -6 to 6
- b_proj: bfloat16 [4096, 1024], P('seq', 'grp'), may hold values from -6 to 6
- c_proj: bfloat16 [4096, 1024], P('seq', 'grp'), may hold values from -0.5 to 0.5
- dt_raw: float32 [4096, 64], P('seq', 'grp'), as said below
- dt_bias: float32 [64], P('grp'), may hold values from -3.5 to -1.5
- a_log: float32 [64], P('grp'), as said below
- skip_d: float32 [64], P('grp'), may hold values from 0.2 to 1
- norm_gain: float32 [8192], P('grp'), may hold values from 0.5 to 1.5
- w_out: bfloat16 [8192, 8192], P('grp', 'seq'), may hold values from -0.03125 to 0.03125
Outputs:
- mixed: bfloat16 [4096, 8192], P('seq', 'grp')
Inputs may be any that keep to these rules, and one draw needn't show every extreme that they name: `dt_raw`: step size offsets, with bursts at a few positions of the sequence shared by all heads. `a_log`: log decay rates per head, between log(0.1 / (0.08 * 4096)) and log(0.6).
All inputs are finite; a program needn't handle non-finite values.
Results may differ from a plain program's by a relative error of at most 0.0049.
Values may be sent and summed in bfloat16 or wider, within the bound.
A program may use at most 128 MiB of HBM per device.

v0:
```python
import math

import jax
import jax.numpy as jnp
from jax import lax
from jax.sharding import PartitionSpec as P

CHANNEL_WIDTH = 128
STATE = 128


HIGH = lax.Precision.HIGHEST


def prefix(array, axis, combine, identity):
    length, mine = (lax.axis_size(axis), lax.axis_index(axis))
    everything = jax.tree.map(lambda part: lax.all_gather(part, axis), array)
    start = jax.tree.map(
        lambda part, zero: jnp.broadcast_to(jnp.asarray(zero, part.dtype), part.shape),
        array,
        identity,
    )

    def turn(k, before):
        reached = k < mine
        new = combine(before, jax.tree.map(lambda part: part[k], everything))
        return jax.tree.map(lambda a, b: jnp.where(reached, a, b), new, before)

    return lax.fori_loop(0, length, turn, start)


def ssd_blocks(xf, dt, la, bm, cm, braw, craw, init):
    length, heads, width = xf.shape
    groups = bm.shape[1]
    ratio = heads // groups
    block = math.gcd(length, 256)
    count = length // block

    def step(state, blk):
        xb, dtb, lab, bb, cb, bnar, cnar = blk
        cum = jnp.cumsum(lab, axis=0)
        attention_logits = jnp.einsum(
            "tgn,sgn->gts", cnar, bnar, preferred_element_type=jnp.float32
        )
        attention_logits = jnp.repeat(attention_logits, ratio, axis=0)
        diff = cum.T[:, :, None] - cum.T[:, None, :]
        rows = lax.broadcasted_iota(jnp.int32, (block, block), 0)
        cols = lax.broadcasted_iota(jnp.int32, (block, block), 1)
        mask = (rows >= cols)[None, :, :]
        decay = jnp.exp(jnp.where(mask, diff, -1e30))
        mixing = decay * attention_logits * dtb.T[:, None, :]
        outs = jnp.einsum("hts,shp->thp", mixing, xb, precision=HIGH)
        cheads = jnp.repeat(cb, ratio, axis=1)
        incoming_channel_bundles = jnp.repeat(bb, ratio, axis=1)
        outs = outs + jnp.exp(cum)[:, :, None] * jnp.einsum(
            "thn,hpn->thp", cheads, state, precision=HIGH
        )
        weights = jnp.exp(cum[-1][None, :] - cum) * dtb
        fresh = jnp.einsum("sh,shp,shn->hpn", weights, xb, incoming_channel_bundles, precision=HIGH)
        state = jnp.exp(cum[-1])[:, None, None] * state + fresh
        return (state, outs)

    blocks = (
        xf.reshape(count, block, heads, width),
        dt.reshape(count, block, heads),
        la.reshape(count, block, heads),
        bm.reshape(count, block, groups, -1),
        cm.reshape(count, block, groups, -1),
        braw.reshape(count, block, groups, -1),
        craw.reshape(count, block, groups, -1),
    )
    final, outs = lax.scan(step, init, blocks)
    return (outs.reshape(length, heads, width), final, jnp.sum(la, axis=0))


def gated_norm_output(y, multiplier_channels, norm_gain, groups):
    length = y.shape[0]
    gated = y.reshape(length, -1) * jax.nn.silu(multiplier_channels.astype(jnp.float32))
    split = gated.reshape(length, groups, -1)
    split = split * lax.rsqrt(jnp.mean(split * split, axis=-1, keepdims=True) + 1e-05)
    return (split.reshape(length, -1) * norm_gain).astype(jnp.bfloat16)


def combine_states(earlier_state, later):
    return (earlier_state[0] * later[0], later[0][:, None, None] * earlier_state[1] + later[1])


def shards(
    x_in, multiplier_channels, b_proj, c_proj, dt_raw, dt_bias, a_log, skip_d, norm_gain, w_out
):
    length = x_in.shape[0]
    heads = dt_raw.shape[1]
    groups = b_proj.shape[1] // STATE
    xf = x_in.astype(jnp.float32).reshape(length, heads, CHANNEL_WIDTH)
    dt = jax.nn.softplus(dt_raw + dt_bias)
    la = -jnp.exp(a_log) * dt
    braw = b_proj.reshape(length, groups, STATE)
    craw = c_proj.reshape(length, groups, STATE)
    bm = braw.astype(jnp.float32)
    cm = craw.astype(jnp.float32)
    empty = jnp.zeros((heads, CHANNEL_WIDTH, STATE), jnp.float32)
    y, local_end, total = ssd_blocks(xf, dt, la, bm, cm, braw, craw, empty)
    identity = (jnp.ones((heads,), jnp.float32), empty)
    carried = prefix((jnp.exp(total), local_end), "seq", combine_states, identity)
    cum = jnp.cumsum(la, axis=0)
    cheads = jnp.repeat(cm, heads // groups, axis=1)
    y = y + jnp.exp(cum)[:, :, None] * jnp.einsum(
        "thn,hpn->thp", cheads, carried[1], precision=HIGH
    )
    y = y + skip_d[None, :, None] * xf
    normed = gated_norm_output(y, multiplier_channels, norm_gain, groups)
    partial_out = jnp.dot(
        normed, lax.all_gather(w_out, "seq", axis=1, tiled=True), preferred_element_type=jnp.float32
    )
    return lax.psum_scatter(partial_out, "grp", scatter_dimension=1, tiled=True).astype(
        jnp.bfloat16
    )


def solution(mesh):
    return jax.shard_map(
        shards,
        mesh=mesh,
        in_specs=(
            P("seq", "grp"),
            P("seq", "grp"),
            P("seq", "grp"),
            P("seq", "grp"),
            P("seq", "grp"),
            P("grp"),
            P("grp"),
            P("grp"),
            P("grp"),
            P("grp", "seq"),
        ),
        out_specs=P("seq", "grp"),
        check_vma=False,
    )
```

profile of v0, /device:TPU:4, one launch (start us, length us, event | category | flops | bytes accessed | tf_op | source)
XLA Modules:
  0.0 358.2 jit_solution(16501429066232339684)
XLA Ops:
  11.2 1.4 convolution_add_fusion
  14.4 1.3 dynamic-slice.6
  16.4 78.6 %all-reduce = f32[256]{0:T(256)S(1)} all-reduce(f32[256]{0:T(256)S(1)} %exponential_dynamic-update-slice_fusion), channel_id=2, replica_groups=mesh['seq'=32,'grp'=8] {'seq'}, use_global_device_ids=true, to_apply=%add | all-reduce | flops 256 | bytes 2048
  96.8 1.2 fusion.5
  98.0 58.5 %all-gather.7.cloned.1.call-done = f32[256,128,128]{2,1,0:T(8,128)} async-done(((f32[8,128,128]{2,1,0:T(8,128)}), f32[256,128,128]{2,1,0:T(8,128)}) %all-gather.7.cloned.1.call-update) | async-done | bytes 16777232 | tf_op jit(solution)/shard_map/all_gather | solution.py:17
  156.5 39.0 %while.9 = (s32[]{:T(128)}, f32[8,128,128]{2,1,0:T(8,128)S(1)}, s32[]{:T(128)}, f32[32,8]{1,0:T(8,128)S(1)}, f32[32,8,128,128]{3,2,1,0:T(8,128)}, /*index=5*/s32[]{:T(128)}, s32[]{:T(128)}) while((s32[]{:T(128)}, f32[8,128,128]{2,1,0:T(8,128)S(1)}, s32[]{:T(128)}, f32[32,8]{1,0:T(8,128)S(1)}, f32[32,8,128,128]{3,2,1,0:T(8,128)}, ...), condition=%wide.region_3.4_spmd.clone, body=%wide.region_2.3_spmd.clone.sunk | while | flops 524292 | bytes 1573065 | solution.py:29
  160.1 1.2 fusion.41
  161.3 1.2 fusion.41
  162.5 1.2 fusion.41
  167.4 1.2 fusion.41
  168.6 1.2 fusion.41
  169.9 1.2 fusion.41
  176.0 1.2 fusion.41
  177.2 1.2 fusion.41
  183.3 1.2 fusion.41
  184.5 1.2 fusion.41
  188.2 1.2 fusion.41
  189.4 1.2 fusion.41
  193.1 1.2 fusion.41
  195.5 1.9 fusion.3
  197.8 109.3 %all-gather.5.cloned.1.call-done = bf16[1024,8192]{1,0:T(8,128)(2,1)} async-done(((bf16[1024,256]{1,0:T(8,128)(2,1)}), bf16[1024,8192]{1,0:T(8,128)(2,1)}) %all-gather.5.cloned.1.call-update) | async-done | bytes 16777232 | tf_op jit(solution)/shard_map/all_gather | solution.py:113
  307.1 10.2 %fusion.15 = f32[128,8192]{1,0:T(8,128)} fusion(bf16[1024,8192]{1,0:T(8,128)(2,1)} %all-gather.5.cloned.1.call-done, f32[1024]{0:T(1024)S(1)} %copy-done.1, f32[128]{0:T(128)S(1)} %add_rsqrt_fusion, f32[128,1024]{1,0:T(8,128)S(1)} %copy.41, bf16[128,1024]{1,0:T(8,128)(2,1)S(1)} %copy-done), kind=kOutput, calls=%fused_computation.27 | convolution fusion | flops 2148663296 | bytes 21762560 | tf_op jit(solution)/shard_map/dot_general | solution.py:112
  317.3 32.7 %reduce-scatter.2.cloned.1.call-done = f32[128,1024]{1,0:T(8,128)} async-done(((f32[128,8192]{1,0:T(8,128)}), f32[128,1024]{1,0:T(8,128)}) %reduce-scatter.2.cloned.1.call-update) | async-done | bytes 524304 | tf_op jit(solution)/shard_map/reduce_scatter | solution.py:115
  349.9 1.8 convert_element_type.22
  (85 shorter events, 31.3 us)
Async XLA Ops:
  6.5 191.0 %copy-start = (bf16[128,1024]{1,0:T(8,128)(2,1)S(1)}, bf16[128,1024]{1,0:T(8,128)(2,1)}, u32[]{:S(2)}) copy-start(bf16[128,1024]{1,0:T(8,128)(2,1)} %param.13) | copy-start | bytes 786436
  6.5 300.5 %copy-start.1 = (f32[1024]{0:T(1024)S(1)}, f32[1024]{0:T(1024)}, u32[]{:S(2)}) copy-start(f32[1024]{0:T(1024)} %param.20) | copy-start | bytes 12292
  6.5 149.9 %all-gather.7.cloned.1.call-start = ((), (), s32[]{:S(2)}) async-start(), calls=%async_computation.3 | async-start | bytes 17301504 | tf_op jit(solution)/shard_map/all_gather | solution.py:17
  12.6 294.5 %all-gather.5.cloned.1.call-start = ((), (), s32[]{:S(2)}) async-start(), calls=%async_computation.1 | async-start | bytes 17301504 | tf_op jit(solution)/shard_map/all_gather | solution.py:113
  13.4 336.6 %reduce-scatter.2.cloned.1.call-start = ((), (), s32[]{:S(2)}) async-start(), calls=%async_computation.2 | async-start | bytes 4718592 | tf_op jit(solution)/shard_map/reduce_scatter | solution.py:115
Sparse Core Ops, SparseCore 0:
  12.7 143.6 all-gather.6
  158.9 148.0 all-gather.4
  317.4 32.5 reduce-scatter.1
where the time goes:
time: 365 us; the launch traced here: 358 us
  waiting for transfers between devices  201 us (55%)
  blocking collectives  78.6 us (22%)
  other arithmetic  43.9 us (12%)
  matrix products  16.4 us (4%)
  between operations  13.9 us (4%)
    all_gather x1, waiting for transfers between devices, shards(): lax.all_gather(w_out, 'seq', axis=1, tiled=True)  109 us
    unnamed x1, blocking collectives  78.6 us
    all_gather x1, waiting for transfers between devices, prefix(): everything = jax.tree.map(lambda part: lax.all_gather(part, axis), array)  58.5 us
    select_n x32, other arithmetic, turn(): return jax.tree.map(lambda a, b: jnp.where(reached, a, b), new, before)  37.7 us
    reduce_scatter x1, waiting for transfers between devices, shards(): lax.psum_scatter(partial_out, 'grp', scatter_dimension=1, tiled=True)  32.7 us
    dot_general x1, matrix products, shards(): jnp.dot(normed, lax.all_gather(w_out, 'seq', axis=1, tiled=True), preferr...  10.2 us
  transfers between devices with their start and end apart: 3, of which 3 were waited for; matrix products, arithmetic and copies ran while one was open for 13% of the time, Pallas kernels for 0%

commit v1 on v0

v1 whole, which is shorter than its diff:
```python
import jax
import jax.numpy as jnp
from jax import lax
from jax.experimental import pallas as pl
from jax.experimental.pallas import tpu as pltpu
from jax.sharding import PartitionSpec as P

MESH = pl.DeviceIdType.MESH
HIGH = lax.Precision.HIGHEST
WIDTH = 128
STATE = 128
NZ, NY, NX, NC = 8, 4, 4, 2
F32 = jnp.float32
BF16 = jnp.bfloat16


def split(value):
    high = value.astype(BF16)
    return high, (value - high.astype(F32)).astype(BF16)


def dot(a, b, dims=((1,), (0,))):
    return lax.dot_general(a, b, (dims, ((), ())), preferred_element_type=F32)


def kernel(
    x_ref, m_ref, b_ref, c_ref, dt_ref, bias_ref, alog_ref, skip_ref, gain_ref, w_ref,
    out_ref,
    wall, abuf, ybuf, smbuf, qbuf,
    lsend, lrecv, tsend, trecv,
    rsend, rrecv, dsend, drecv,
    esend, erecv, ssend, srecv,
    psend, precv, keep, rssend, rsrecv, fsend,
    w_local, w_ss, w_rs, l_ss, l_rs, t_ss, t_rs, r_ss, r_rs, d_ss, d_rs,
    e_ss, e_rs, s_ss, s_rs, a_ss, a_rs, p_ss, p_rs, x_ss, x_rs, f_ss, f_rs,
):
    seq, grp = lax.axis_index("seq"), lax.axis_index("grp")
    z, y = seq // NY, seq % NY
    x, core = grp // NC, grp % NC
    tokens, channels = x_ref.shape
    heads = channels // WIDTH
    pair = channels // NY
    cols = w_ref.shape[1]
    khalf = w_ref.shape[0] // 2
    thalf = tokens // 2

    def device(dz=0, dy=0, dx=0, dc=0):
        return (
            ((z + dz) % NZ) * NY + (y + dy) % NY,
            ((x + dx) % NX) * NC + (core + dc) % NC,
        )

    def remote(src, dst, ss, rs, to):
        return pltpu.make_async_remote_copy(
            src_ref=src, dst_ref=dst, send_sem=ss, recv_sem=rs, device_id=to, device_id_type=MESH
        )

    sends = []

    def send(src, dst, ss, rs, to):
        copy = remote(src, dst, ss, rs, to)
        copy.start()
        sends.append(copy)

    def arrived(dst, ss, rs):
        remote(dst, dst, ss, rs, device(dz=1)).wait_recv()

    barrier = pltpu.get_barrier_semaphore()
    others = (
        [dict(dz=k) for k in range(1, NZ)]
        + [dict(dy=k) for k in range(1, NY)]
        + [dict(dx=k) for k in range(1, NX)]
        + [dict(dc=1)]
    )
    for other in others:
        pl.semaphore_signal(barrier, inc=1, device_id=device(**other), device_id_type=MESH)

    raw = dt_ref[...] + bias_ref[...]
    dt = jnp.maximum(raw, 0.0) + jnp.log1p(jnp.exp(-jnp.abs(raw)))
    la = -jnp.exp(alog_ref[...]) * dt
    rows = lax.broadcasted_iota(jnp.int32, (tokens, tokens), 0)
    columns = lax.broadcasted_iota(jnp.int32, (tokens, tokens), 1)
    mask = rows >= columns
    cum = lax.dot_general(
        mask.astype(F32), la, (((1,), (0,)), ((), ())), precision=HIGH, preferred_element_type=F32
    )
    total = cum[tokens - 1 : tokens, :]
    weight = jnp.exp(total - cum) * dt

    pl.semaphore_wait(barrier, len(others))

    own_w = pltpu.make_async_copy(w_ref, wall.at[z], w_local)
    own_w.start()

    def w_part(origin, half):
        return wall.at[origin, pl.ds(half * khalf, khalf), :]

    for i in range(2):
        for d, sign in enumerate((1, -1)):
            half = i if d == 0 else 1 - i
            send(
                w_ref.at[pl.ds(half * khalf, khalf), :],
                w_part(z, half),
                w_ss.at[d, 0, i],
                w_rs.at[d, 0, i],
                device(dz=sign),
            )

    def relay(step, i):
        for d, sign in enumerate((1, -1)):
            half = i if d == 0 else 1 - i
            origin = (z - sign * step) % NZ
            arrived(w_part(origin, half), w_ss.at[d, step - 1, i], w_rs.at[d, step - 1, i])
            if step < NZ // 2 - 1 or (step == NZ // 2 - 1 and i == 0):
                send(
                    w_part(origin, half),
                    w_part(origin, half),
                    w_ss.at[d, step, i],
                    w_rs.at[d, step, i],
                    device(dz=sign),
                )

    bmat, cmat = b_ref[...], c_ref[...]
    for j in range(NY):
        parts = []
        for h in range(j * heads // NY, (j + 1) * heads // NY):
            xh = x_ref[:, h * WIDTH : (h + 1) * WIDTH].astype(F32)
            parts.append(xh * weight[:, h : h + 1])
        high, low = split(jnp.concatenate(parts, axis=1))
        state = dot(bmat, high, ((0,), (0,))) + dot(bmat, low, ((0,), (0,)))
        lsend[j] = state.astype(BF16)
        tsend[j] = jnp.concatenate(
            [
                jnp.broadcast_to(total[:, h : h + 1], (8, WIDTH))
                for h in range(j * heads // NY, (j + 1) * heads // NY)
            ],
            axis=1,
        )
    for k in range(1, NY):
        to = (y + k) % NY
        send(lsend.at[to], lrecv.at[y], l_ss.at[k - 1], l_rs.at[k - 1], device(dy=k))
        send(tsend.at[to], trecv.at[y], t_ss.at[k - 1], t_rs.at[k - 1], device(dy=k))
    lrecv[y] = lsend[y]
    trecv[y] = tsend[y]

    logits = dot(cmat, bmat, ((1,), (1,)))
    cum_t = jnp.transpose(cum)
    dt_t = jnp.transpose(dt)
    for h in range(heads):
        span = slice(h * WIDTH, (h + 1) * WIDTH)
        decay = jnp.exp(jnp.where(mask, cum[:, h : h + 1] - cum_t[h : h + 1, :], -1e30))
        high, low = split(decay * logits * dt_t[h : h + 1, :])
        xh = x_ref[:, span]
        ybuf[:, span] = dot(high, xh) + dot(low, xh) + skip_ref[:, h : h + 1] * xh.astype(F32)
        gate = m_ref[:, span].astype(F32)
        smbuf[:, span] = gate / (1.0 + jnp.exp(-gate))
    relay(1, 0)

    for k in range(1, NY):
        source = (y - k) % NY
        arrived(lrecv.at[source], l_ss.at[k - 1], l_rs.at[k - 1])
        arrived(trecv.at[source], t_ss.at[k - 1], t_rs.at[k - 1])
    before = [jnp.zeros((1, pair), F32)]
    current = lrecv[0].astype(F32)
    for j in range(NY):
        before.append(before[-1] + trecv[j][0:1, :])
        if j:
            current = jnp.exp(trecv[j][0:1, :]) * current + lrecv[j].astype(F32)
    size = STATE // NZ
    for k in range(NZ):
        rsend[k] = current[k * size : (k + 1) * size, :].astype(BF16)
    dsend[...] = jnp.broadcast_to(before[NY], (8, pair))
    for k in range(1, NZ):
        to = (z + k) % NZ
        send(rsend.at[to], rrecv.at[z], r_ss.at[k - 1], r_rs.at[k - 1], device(dz=k))
        send(dsend, drecv.at[z], d_ss.at[k - 1], d_rs.at[k - 1], device(dz=k))
    rrecv[z] = rsend[z]
    drecv[z] = dsend[...]
    current = lrecv[0].astype(F32)
    for j in range(1, NY):
        qbuf[j - 1] = current
        if j < NY - 1:
            current = jnp.exp(trecv[j][0:1, :]) * current + lrecv[j].astype(F32)
    relay(1, 1)

    for k in range(1, NZ):
        source = (z - k) % NZ
        arrived(rrecv.at[source], r_ss.at[k - 1], r_rs.at[k - 1])
        arrived(drecv.at[source], d_ss.at[k - 1], d_rs.at[k - 1])
    current = jnp.zeros((size, pair), F32)
    for k in range(NZ):
        esend[k] = current.astype(BF16)
        current = jnp.exp(drecv[k][0:1, :]) * current + rrecv[k].astype(F32)
    for k in range(1, NZ):
        to = (z + k) % NZ
        send(esend.at[to], erecv.at[z], e_ss.at[k - 1], e_rs.at[k - 1], device(dz=k))
    erecv[z] = esend[z]
    relay(2, 0)
    for k in range(1, NZ):
        source = (z - k) % NZ
        arrived(erecv.at[source], e_ss.at[k - 1], e_rs.at[k - 1])
    entry = jnp.concatenate([erecv[k].astype(F32) for k in range(NZ)], axis=0)
    ssend[0] = entry.astype(BF16)
    for j in range(1, NY):
        ssend[j] = (qbuf[j - 1] + jnp.exp(before[j]) * entry).astype(BF16)
    for k in range(1, NY):
        to = (y + k) % NY
        send(ssend.at[to], srecv.at[y], s_ss.at[k - 1], s_rs.at[k - 1], device(dy=k))
    srecv[y] = ssend[y]
    relay(2, 1)
    for k in range(1, NY):
        source = (y - k) % NY
        arrived(srecv.at[source], s_ss.at[k - 1], s_rs.at[k - 1])

    grown = jnp.exp(cum)
    squares = jnp.zeros((tokens, WIDTH), F32)
    for j in range(NY):
        inter = dot(cmat, srecv[j])
        for i in range(heads // NY):
            h = j * heads // NY + i
            span = slice(h * WIDTH, (h + 1) * WIDTH)
            value = ybuf[:, span] + grown[:, h : h + 1] * inter[:, i * WIDTH : (i + 1) * WIDTH]
            value = value * smbuf[:, span]
            ybuf[:, span] = value
            squares = squares + value * value
    mean = jnp.sum(squares, axis=1, keepdims=True) * (1.0 / channels)
    scale = lax.rsqrt(mean + 1e-05)
    abuf[y] = (ybuf[...] * scale * gain_ref[...]).astype(BF16)

    def a_part(origin, half):
        return abuf.at[origin, pl.ds(half * thalf, thalf), :]

    for i in range(2):
        for d, sign in enumerate((1, -1)):
            half = i if d == 0 else 1 - i
            part = a_part(y, half)
            send(part, part, a_ss.at[d, i], a_rs.at[d, i], device(dy=sign))
    relay(3, 0)
    for d, sign in enumerate((1, -1)):
        origin = (y - sign) % NY
        half = d
        part = a_part(origin, half)
        arrived(part, a_ss.at[d, 0], a_rs.at[d, 0])
        send(part, part, a_ss.at[d, 2], a_rs.at[d, 2], device(dy=sign))
    relay(3, 1)
    own_w.wait()
    relay(4, 0)

    turns = (0, -1, 1, 2)

    def multiply(t):
        if t == 0:
            pass
        elif t < 3:
            d = t - 1
            arrived(a_part((y + turns[t]) % NY, 1 - d), a_ss.at[d, 1], a_rs.at[d, 1])
        else:
            for d in range(2):
                arrived(a_part((y + 2) % NY, d), a_ss.at[d, 2], a_rs.at[d, 2])
        a = abuf[(y + turns[t]) % NY]
        for k in (2, 1, 3, 0):
            q = (x + k) % NX
            psend[t, k] = dot(a, wall[q * NC + 1 - core]).astype(BF16)
            send(psend.at[t, k], precv.at[t, k], p_ss.at[t, k], p_rs.at[t, k], device(dc=1))
            keep[t, k] = dot(a, wall[q * NC + core])

    def chip_sum(t):
        for k in (2, 1, 3, 0):
            arrived(precv.at[t, k], p_ss.at[t, k], p_rs.at[t, k])
            both = keep[t, k] + precv[t, k].astype(F32)
            if k:
                rssend[t, k - 1] = both.astype(BF16)
                send(
                    rssend.at[t, k - 1],
                    rsrecv.at[t, k - 1],
                    x_ss.at[t, k - 1],
                    x_rs.at[t, k - 1],
                    device(dx=k),
                )
            else:
                keep[t, k] = both

    mine = pl.ds(pl.multiple_of(y * cols, cols), cols)

    def finish(t):
        value = keep[t, 0]
        for k in range(1, NX):
            arrived(rsrecv.at[t, k - 1], x_ss.at[t, k - 1], x_rs.at[t, k - 1])
            value = value + rsrecv[t, k - 1].astype(F32)
        if t == 0:
            out_ref[:, mine] = value.astype(BF16)
        else:
            fsend[t - 1] = value.astype(BF16)
            send(
                fsend.at[t - 1],
                out_ref.at[:, mine],
                f_ss.at[t - 1],
                f_rs.at[t - 1],
                device(dy=turns[t]),
            )

    for t in range(NY + 2):
        if t < NY:
            multiply(t)
        if 1 <= t <= NY:
            chip_sum(t - 1)
        if t >= 2:
            finish(t - 2)
    for t in range(1, NY):
        source = (y - turns[t]) % NY
        span = pl.ds(pl.multiple_of(source * cols, cols), cols)
        arrived(out_ref.at[:, span], f_ss.at[t - 1], f_rs.at[t - 1])
    for copy in sends:
        copy.wait_send()


def shards(
    x_in, multiplier_channels, b_proj, c_proj, dt_raw, dt_bias, a_log, skip_d, norm_gain, w_out
):
    tokens, channels = x_in.shape
    depth, cols = w_out.shape
    pair = channels // NY
    size = STATE // NZ
    vmem = pl.BlockSpec(memory_space=pltpu.VMEM)
    dma = pltpu.SemaphoreType.DMA
    scratch = [
        pltpu.VMEM((NZ, depth, cols), BF16),
        pltpu.VMEM((NY, tokens, channels), BF16),
        pltpu.VMEM((tokens, channels), F32),
        pltpu.VMEM((tokens, channels), F32),
        pltpu.VMEM((NY - 1, STATE, pair), F32),
        pltpu.VMEM((NY, STATE, pair), BF16),
        pltpu.VMEM((NY, STATE, pair), BF16),
        pltpu.VMEM((NY, 8, pair), F32),
        pltpu.VMEM((NY, 8, pair), F32),
        pltpu.VMEM((NZ, size, pair), BF16),
        pltpu.VMEM((NZ, size, pair), BF16),
        pltpu.VMEM((8, pair), F32),
        pltpu.VMEM((NZ, 8, pair), F32),
        pltpu.VMEM((NZ, size, pair), BF16),
        pltpu.VMEM((NZ, size, pair), BF16),
        pltpu.VMEM((NY, STATE, pair), BF16),
        pltpu.VMEM((NY, STATE, pair), BF16),
        pltpu.VMEM((NY, NX, tokens, cols), BF16),
        pltpu.VMEM((NY, NX, tokens, cols), BF16),
        pltpu.VMEM((NY, NX, tokens, cols), F32),
        pltpu.VMEM((NY, NX - 1, tokens, cols), BF16),
        pltpu.VMEM((NY, NX - 1, tokens, cols), BF16),
        pltpu.VMEM((NY - 1, tokens, cols), BF16),
        dma,
        dma((2, 4, 2)), dma((2, 4, 2)),
        dma((3,)), dma((3,)), dma((3,)), dma((3,)),
        dma((7,)), dma((7,)), dma((7,)), dma((7,)),
        dma((7,)), dma((7,)),
        dma((3,)), dma((3,)),
        dma((2, 3)), dma((2, 3)),
        dma((4, 4)), dma((4, 4)),
        dma((4, 3)), dma((4, 3)),
        dma((3,)), dma((3,)),
    ]
    return pl.pallas_call(
        kernel,
        out_shape=jax.ShapeDtypeStruct((tokens, channels), BF16),
        in_specs=[vmem] * 9 + [pl.BlockSpec(memory_space=pl.ANY)],
        out_specs=vmem,
        scratch_shapes=scratch,
        compiler_params=pltpu.CompilerParams(
            collective_id=0, has_side_effects=True, vmem_limit_bytes=56 * 1024 * 1024
        ),
        name="mixer",
    )(
        x_in,
        multiplier_channels,
        b_proj,
        c_proj,
        dt_raw,
        dt_bias.reshape(1, -1),
        a_log.reshape(1, -1),
        skip_d.reshape(1, -1),
        norm_gain.reshape(1, -1),
        w_out,
    )


def solution(mesh):
    return jax.shard_map(
        shards,
        mesh=mesh,
        in_specs=(
            P("seq", "grp"),
            P("seq", "grp"),
            P("seq", "grp"),
            P("seq", "grp"),
            P("seq", "grp"),
            P("grp"),
            P("grp"),
            P("grp"),
            P("grp"),
            P("grp", "seq"),
        ),
        out_specs=P("seq", "grp"),
        check_vma=False,
    )
```

time: 365 us -> 81.6 us (0.22); the launches traced: 358 us -> 80.7 us
  waiting for transfers between devices: 201 us -> 0 us
  blocking collectives: 78.6 us -> 0 us
  Pallas kernels: 0 us -> 77.6 us
  other arithmetic: 43.9 us -> 0 us
  matrix products: 16.4 us -> 0 us
  between operations: 13.9 us -> 0.01 us
    all_gather x2 -> x0, waiting for transfers between devices: 168 us -> none  [the longest x1 109 us: shards(): lax.all_gather(w_out, 'seq', axis=1, tiled=True)]
    unnamed x1 -> x0, blocking collectives: 78.6 us -> none
    pallas_call x0 -> x1, Pallas kernels: none -> 77.6 us  [shards(): pl.pallas_call(kernel, out_shape=jax.ShapeDtypeStruct((tokens, channels),...]
    select_n x32 -> x0, other arithmetic: 37.7 us -> none  [turn(): return jax.tree.map(lambda a, b: jnp.where(reached, a, b), new, before)]
    reduce_scatter x1 -> x0, waiting for transfers between devices: 32.7 us -> none  [shards(): lax.psum_scatter(partial_out, 'grp', scatter_dimension=1, tiled=True)]
    dot_general x6 -> x0, matrix products: 16.4 us -> none  [the longest x1 10.2 us: shards(): jnp.dot(normed, lax.all_gather(w_out, 'seq', axis=1, tiled=True), preferr...]
  transfers between devices with their start and end apart: 3 -> 0, of which waited for: 3 -> 0; matrix products, arithmetic and copies ran while one was open for 13% -> 0% of each run, Pallas kernels for 0% -> 0%
where the time goes in v1:
time: 81.6 us; the launch traced here: 80.7 us
  Pallas kernels  77.6 us (95%)
  local copies, waits for them, and re-layouts  3.08 us (4%)
    pallas_call x1, Pallas kernels, shards(): pl.pallas_call(kernel, out_shape=jax.ShapeDtypeStruct((tokens, channels),...  77.6 us
    unnamed x4, local copies, waits for them, and re-layouts  3.08 us

profile of v1, /device:TPU:4, one launch (start us, length us, event | category | flops | bytes accessed | tf_op | source)
XLA Modules:
  0.0 80.7 jit_solution(18154567775806057796)
XLA Ops:
  0.0 0.0 copy-start
  0.0 0.7 copy-done
  0.7 0.7 copy.11.dt_ref
  1.4 77.6 %mixer.1 = bf16[128,1024]{1,0:T(8,128)(2,1)} custom-call(bf16[128,1024]{1,0:T(8,128)(2,1)} %x_ref.1, bf16[128,1024]{1,0:T(8,128)(2,1)} %m_ref.1, bf16[128,128]{1,0:T(8,128)(2,1)} %b_ref.1, bf16[128,128]{1,0:T(8,128)(2,1)} %c_ref.1, f32[128,8]{1,0:T(8,128)} %copy.11.dt_ref, f32[1,8]{1,0:T(1,128)} %bitcast.5, f32[1,8]{1,0:T(1,128)} %bitcast.6, ...), custom_call_target="tpu_custom_call" | custom-call | tf_op jit(solution)/shard_map/mixer/pallas_call | solution.py:361
  79.0 1.7 %copy.13 = bf16[128,1024]{1,0:T(8,128)(2,1)} copy(bf16[128,1024]{1,0:T(8,128)(2,1)} %mixer.1) | data formatting | bytes 524288
Async XLA Ops:
  0.0 0.7 copy-start

commit v2 on v1

v2 whole, which is shorter than its diff:
```python
import jax
import jax.numpy as jnp
from jax import lax
from jax.experimental import pallas as pl
from jax.experimental.pallas import tpu as pltpu
from jax.sharding import PartitionSpec as P

MESH = pl.DeviceIdType.MESH
HIGH = lax.Precision.HIGHEST
WIDTH = 128
STATE = 128
NZ, NY, NX, NC = 8, 4, 4, 2
F32 = jnp.float32
BF16 = jnp.bfloat16


def split(value):
    high = value.astype(BF16)
    return high, (value - high.astype(F32)).astype(BF16)


def dot(a, b, dims=((1,), (0,))):
    return lax.dot_general(a, b, (dims, ((), ())), preferred_element_type=F32)


def kernel(
    dt_ref, bias_ref, alog_ref, skip_ref, gain_ref, b_ref, c_ref, x_ref, m_ref, w_ref,
    out_ref,
    wall, abuf, ybuf, smbuf, qbuf,
    lsend, lrecv, tsend, trecv,
    rsend, rrecv, dsend, drecv,
    esend, erecv, ssend, srecv,
    pgive, precv, pkeep, xsend, xrecv, fsend,
    w_local, w_ss, w_rs, l_ss, l_rs, t_ss, t_rs, r_ss, r_rs, d_ss, d_rs,
    e_ss, e_rs, s_ss, s_rs, a_ss, a_rs, p_ss, p_rs, x_ss, x_rs, f_ss, f_rs,
):
    seq, grp = lax.axis_index("seq"), lax.axis_index("grp")
    z, y = seq // NY, seq % NY
    x, core = grp // NC, grp % NC
    tokens, channels = x_ref.shape
    heads = channels // WIDTH
    pair = channels // NY
    cols = w_ref.shape[1]
    khalf = w_ref.shape[0] // 2
    chalf = cols // 2
    thalf = tokens // 2
    share = NY * tokens // NC

    def device(dz=0, dy=0, dx=0, dc=0):
        return (
            ((z + dz) % NZ) * NY + (y + dy) % NY,
            ((x + dx) % NX) * NC + (core + dc) % NC,
        )

    def remote(src, dst, ss, rs, to):
        return pltpu.make_async_remote_copy(
            src_ref=src, dst_ref=dst, send_sem=ss, recv_sem=rs, device_id=to, device_id_type=MESH
        )

    sends = []

    def send(src, dst, ss, rs, to):
        copy = remote(src, dst, ss, rs, to)
        copy.start()
        sends.append(copy)

    def arrived(dst, ss, rs):
        remote(dst, dst, ss, rs, device(dz=1)).wait_recv()

    barrier = pltpu.get_barrier_semaphore()
    others = (
        [dict(dz=k) for k in range(1, NZ)]
        + [dict(dy=k) for k in range(1, NY)]
        + [dict(dx=k, dc=c) for k in range(NX) for c in range(NC) if k or c]
    )
    for other in others:
        pl.semaphore_signal(barrier, inc=1, device_id=device(**other), device_id_type=MESH)
    own_w = []
    for i in range(2):
        copy = pltpu.make_async_copy(
            w_ref.at[:, i * chalf : (i + 1) * chalf], wall.at[z, i], w_local.at[i]
        )
        copy.start()
        own_w.append(copy)

    raw = jnp.transpose(dt_ref[...]) + bias_ref[...]
    dt = jnp.maximum(raw, 0.0) + jnp.log1p(jnp.exp(-jnp.abs(raw)))
    la = -jnp.exp(alog_ref[...]) * dt
    rows = lax.broadcasted_iota(jnp.int32, (tokens, tokens), 0)
    columns = lax.broadcasted_iota(jnp.int32, (tokens, tokens), 1)
    mask = rows >= columns
    cum = lax.dot_general(
        mask.astype(F32), la, (((1,), (0,)), ((), ())), precision=HIGH, preferred_element_type=F32
    )
    total = cum[tokens - 1 : tokens, :]
    weight = jnp.exp(total - cum) * dt

    for copy in own_w:
        copy.wait()
    pl.semaphore_wait(barrier, len(others))

    def w_part(origin, d, i):
        half = i % 2 if d == 0 else 1 - i % 2
        return wall.at[origin, i // 2, pl.ds(half * khalf, khalf), :]

    for i in range(4):
        for d, sign in enumerate((1, -1)):
            part = w_part(z, d, i)
            send(part, part, w_ss.at[d, 0, i], w_rs.at[d, 0, i], device(dz=sign))

    last = NZ // 2
    items = [(step, i) for step in range(1, last) for i in range(4)] + [(last, 0), (last, 2)]
    done = [0]

    def relay(count):
        while done[0] < count:
            step, i = items[done[0]]
            done[0] += 1
            for d, sign in enumerate((1, -1)):
                part = w_part((z - sign * step) % NZ, d, i)
                arrived(part, w_ss.at[d, step - 1, i], w_rs.at[d, step - 1, i])
                if step < last - 1 or (step == last - 1 and i % 2 == 0):
                    send(part, part, w_ss.at[d, step, i], w_rs.at[d, step, i], device(dz=sign))

    bmat, cmat = b_ref[...], c_ref[...]
    for j in range(NY):
        parts = []
        for h in range(j * heads // NY, (j + 1) * heads // NY):
            xh = x_ref[:, h * WIDTH : (h + 1) * WIDTH].astype(F32)
            parts.append(xh * weight[:, h : h + 1])
        high, low = split(jnp.concatenate(parts, axis=1))
        state = dot(bmat, high, ((0,), (0,))) + dot(bmat, low, ((0,), (0,)))
        lsend[j] = state.astype(BF16)
        tsend[j] = jnp.concatenate(
            [
                jnp.broadcast_to(total[:, h : h + 1], (8, WIDTH))
                for h in range(j * heads // NY, (j + 1) * heads // NY)
            ],
            axis=1,
        )
    for k in range(1, NY):
        to = (y + k) % NY
        send(lsend.at[to], lrecv.at[y], l_ss.at[k - 1], l_rs.at[k - 1], device(dy=k))
        send(tsend.at[to], trecv.at[y], t_ss.at[k - 1], t_rs.at[k - 1], device(dy=k))
    lrecv[y] = lsend[y]
    trecv[y] = tsend[y]

    logits = dot(cmat, bmat, ((1,), (1,)))
    cum_t = jnp.transpose(cum)
    dt_t = jnp.transpose(dt)
    for h in range(heads):
        span = slice(h * WIDTH, (h + 1) * WIDTH)
        decay = jnp.exp(jnp.where(mask, cum[:, h : h + 1] - cum_t[h : h + 1, :], -1e30))
        high, low = split(decay * logits * dt_t[h : h + 1, :])
        xh = x_ref[:, span]
        ybuf[:, span] = dot(high, xh) + dot(low, xh) + skip_ref[:, h : h + 1] * xh.astype(F32)
        gate = m_ref[:, span].astype(F32)
        smbuf[:, span] = gate / (1.0 + jnp.exp(-gate))

    for k in range(1, NY):
        source = (y - k) % NY
        arrived(lrecv.at[source], l_ss.at[k - 1], l_rs.at[k - 1])
        arrived(trecv.at[source], t_ss.at[k - 1], t_rs.at[k - 1])
    before = [jnp.zeros((1, pair), F32)]
    current = lrecv[0].astype(F32)
    for j in range(NY):
        before.append(before[-1] + trecv[j][0:1, :])
        if j:
            qbuf[j - 1] = current
            current = jnp.exp(trecv[j][0:1, :]) * current + lrecv[j].astype(F32)
    size = STATE // NZ
    for k in range(NZ):
        rsend[k] = current[k * size : (k + 1) * size, :]
    dsend[...] = jnp.broadcast_to(before[NY], (8, pair))
    for k in range(1, NZ):
        to = (z + k) % NZ
        send(rsend.at[to], rrecv.at[z], r_ss.at[k - 1], r_rs.at[k - 1], device(dz=k))
        send(dsend, drecv.at[z], d_ss.at[k - 1], d_rs.at[k - 1], device(dz=k))
    rrecv[z] = rsend[z]
    drecv[z] = dsend[...]
    relay(2)

    for k in range(1, NZ):
        source = (z - k) % NZ
        arrived(rrecv.at[source], r_ss.at[k - 1], r_rs.at[k - 1])
        arrived(drecv.at[source], d_ss.at[k - 1], d_rs.at[k - 1])
    current = jnp.zeros((size, pair), F32)
    for k in range(NZ):
        esend[k] = current
        current = jnp.exp(drecv[k][0:1, :]) * current + rrecv[k]
    for k in range(1, NZ):
        to = (z + k) % NZ
        send(esend.at[to], erecv.at[z], e_ss.at[k - 1], e_rs.at[k - 1], device(dz=k))
    erecv[z] = esend[z]
    relay(4)
    for k in range(1, NZ):
        source = (z - k) % NZ
        arrived(erecv.at[source], e_ss.at[k - 1], e_rs.at[k - 1])
    entry = jnp.concatenate([erecv[k] for k in range(NZ)], axis=0)
    ssend[0] = entry.astype(BF16)
    for j in range(1, NY):
        ssend[j] = (qbuf[j - 1] + jnp.exp(before[j]) * entry).astype(BF16)
    for k in range(1, NY):
        to = (y + k) % NY
        send(ssend.at[to], srecv.at[y], s_ss.at[k - 1], s_rs.at[k - 1], device(dy=k))
    srecv[y] = ssend[y]
    relay(6)
    for k in range(1, NY):
        source = (y - k) % NY
        arrived(srecv.at[source], s_ss.at[k - 1], s_rs.at[k - 1])

    grown = jnp.exp(cum)
    squares = jnp.zeros((tokens, WIDTH), F32)
    for j in range(NY):
        inter = dot(cmat, srecv[j])
        for i in range(heads // NY):
            h = j * heads // NY + i
            span = slice(h * WIDTH, (h + 1) * WIDTH)
            value = ybuf[:, span] + grown[:, h : h + 1] * inter[:, i * WIDTH : (i + 1) * WIDTH]
            value = value * smbuf[:, span]
            ybuf[:, span] = value
            squares = squares + value * value
    mean = jnp.sum(squares, axis=1, keepdims=True) * (1.0 / channels)
    scale = lax.rsqrt(mean + 1e-05)
    abuf[y] = (ybuf[...] * scale * gain_ref[...]).astype(BF16)

    def a_part(origin, half):
        return abuf.at[origin, pl.ds(half * thalf, thalf), :]

    for i in range(2):
        for d, sign in enumerate((1, -1)):
            part = a_part(y, i if d == 0 else 1 - i)
            send(part, part, a_ss.at[d, i], a_rs.at[d, i], device(dy=sign))
    relay(8)
    for d, sign in enumerate((1, -1)):
        part = a_part((y - sign) % NY, d)
        arrived(part, a_ss.at[d, 0], a_rs.at[d, 0])
        send(part, part, a_ss.at[d, 2], a_rs.at[d, 2], device(dy=sign))
    relay(10)
    for d, sign in enumerate((1, -1)):
        arrived(a_part((y - sign) % NY, 1 - d), a_ss.at[d, 1], a_rs.at[d, 1])
    for d in range(2):
        arrived(a_part((y + 2) % NY, d), a_ss.at[d, 2], a_rs.at[d, 2])

    distances = (0, 1, -1, 2, -2, 3, -3, 4)

    def rows_of(which):
        first = pl.multiple_of(which * (NY // NC), NY // NC)
        return abuf[pl.ds(first, NY // NC)].reshape(share, channels)

    def multiply(n, halves):
        origin = (z + distances[n]) % NZ
        part = jnp.concatenate([wall[origin, i] for i in halves], axis=1)
        give = dot(rows_of(1 - core), part)
        for i in halves:
            first = (i - halves[0]) * chalf
            pgive[n, i] = give[:, first : first + chalf]
            send(pgive.at[n, i], precv.at[n, i], p_ss.at[n, i], p_rs.at[n, i], device(dc=1))
        held = dot(rows_of(core), part)
        for i in halves:
            first = (i - halves[0]) * chalf
            pkeep[n, i] = held[:, first : first + chalf]

    mine = pl.ds(pl.multiple_of(core * share, share), share)

    def owner(n):
        origin = (z + distances[n]) % NZ
        return origin // NC, origin % NC

    def chip_sum(n, halves):
        to_x, to_core = owner(n)
        own = (to_x == x) & (to_core == core)
        for i in halves:
            arrived(precv.at[n, i], p_ss.at[n, i], p_rs.at[n, i])
            both = (pkeep[n, i] + precv[n, i]).astype(BF16)
            xsend[n, i] = both

            @pl.when(own)
            def _():
                xrecv[x, i, mine, :] = xsend[n, i]

            @pl.when(jnp.logical_not(own))
            def _():
                remote(
                    xsend.at[n, i],
                    xrecv.at[x, i, mine, :],
                    x_ss.at[n, i],
                    x_rs.at[x, core, i],
                    (seq, to_x * NC + to_core),
                ).start()

    units = [(n, (0, 1)) for n in range(NZ - 1)] + [(NZ - 1, (0,)), (NZ - 1, (1,))]
    needed = [0, 4, 4, 8, 8, 12, 12, 13, 14]
    for u, (n, halves) in enumerate(units):
        relay(needed[u])
        multiply(n, halves)
        if u:
            chip_sum(*units[u - 1])
    chip_sum(*units[-1])

    for i in range(2):
        for k in range(NX):
            for c in range(NC):
                if k or c:
                    from_x, from_core = (x + k) % NX, (core + c) % NC
                    spot = pl.ds(pl.multiple_of(from_core * share, share), share)
                    arrived(
                        xrecv.at[from_x, i, spot, :], x_ss.at[0, i], x_rs.at[from_x, from_core, i]
                    )
        lanes = pl.ds(pl.multiple_of(y * cols + i * chalf, chalf), chalf)
        for k in (2, 1, 3, 0):
            to = (y + k) % NY
            spot = pl.ds(pl.multiple_of(to * tokens, tokens), tokens)
            value = xrecv[0, i, spot, :].astype(F32)
            for j in range(1, NX):
                value = value + xrecv[j, i, spot, :].astype(F32)
            if k:
                fsend[k - 1, i] = value.astype(BF16)
                send(
                    fsend.at[k - 1, i],
                    out_ref.at[:, lanes],
                    f_ss.at[k - 1, i],
                    f_rs.at[k - 1, i],
                    device(dy=k),
                )
            else:
                out_ref[:, lanes] = value.astype(BF16)
    for i in range(2):
        for k in range(1, NY):
            source = (y - k) % NY
            lanes = pl.ds(pl.multiple_of(source * cols + i * chalf, chalf), chalf)
            arrived(out_ref.at[:, lanes], f_ss.at[k - 1, i], f_rs.at[k - 1, i])
    for copy in sends:
        copy.wait_send()
    for n in range(NZ):
        to_x, to_core = owner(n)

        @pl.when((to_x != x) | (to_core != core))
        def _():
            for i in range(2):
                remote(
                    xsend.at[n, i],
                    xrecv.at[x, i, mine, :],
                    x_ss.at[n, i],
                    x_rs.at[x, core, i],
                    (seq, to_x * NC + to_core),
                ).wait_send()


def shards(
    x_in, multiplier_channels, b_proj, c_proj, dt_raw, dt_bias, a_log, skip_d, norm_gain, w_out
):
    tokens, channels = x_in.shape
    depth, cols = w_out.shape
    pair = channels // NY
    size = STATE // NZ
    vmem = pl.BlockSpec(memory_space=pltpu.VMEM)
    dma = pltpu.SemaphoreType.DMA
    half = cols // 2
    share = NY * tokens // NC
    scratch = [
        pltpu.VMEM((NZ, 2, depth, half), BF16),
        pltpu.VMEM((NY, tokens, channels), BF16),
        pltpu.VMEM((tokens, channels), F32),
        pltpu.VMEM((tokens, channels), F32),
        pltpu.VMEM((NY - 1, STATE, pair), F32),
        pltpu.VMEM((NY, STATE, pair), BF16),
        pltpu.VMEM((NY, STATE, pair), BF16),
        pltpu.VMEM((NY, 8, pair), F32),
        pltpu.VMEM((NY, 8, pair), F32),
        pltpu.VMEM((NZ, size, pair), F32),
        pltpu.VMEM((NZ, size, pair), F32),
        pltpu.VMEM((8, pair), F32),
        pltpu.VMEM((NZ, 8, pair), F32),
        pltpu.VMEM((NZ, size, pair), F32),
        pltpu.VMEM((NZ, size, pair), F32),
        pltpu.VMEM((NY, STATE, pair), BF16),
        pltpu.VMEM((NY, STATE, pair), BF16),
        pltpu.VMEM((NZ, 2, share, half), F32),
        pltpu.VMEM((NZ, 2, share, half), F32),
        pltpu.VMEM((NZ, 2, share, half), F32),
        pltpu.VMEM((NZ, 2, share, half), BF16),
        pltpu.VMEM((NX, 2, NY * tokens, half), BF16),
        pltpu.VMEM((NY - 1, 2, tokens, half), BF16),
        dma((2,)),
        dma((2, 4, 4)), dma((2, 4, 4)),
        dma((3,)), dma((3,)), dma((3,)), dma((3,)),
        dma((7,)), dma((7,)), dma((7,)), dma((7,)),
        dma((7,)), dma((7,)),
        dma((3,)), dma((3,)),
        dma((2, 3)), dma((2, 3)),
        dma((NZ, 2)), dma((NZ, 2)),
        dma((NZ, 2)), dma((NX, NC, 2)),
        dma((NY - 1, 2)), dma((NY - 1, 2)),
    ]
    return pl.pallas_call(
        kernel,
        out_shape=jax.ShapeDtypeStruct((tokens, channels), BF16),
        in_specs=[vmem] * 9 + [pl.BlockSpec(memory_space=pl.ANY)],
        out_specs=vmem,
        scratch_shapes=scratch,
        compiler_params=pltpu.CompilerParams(
            collective_id=0, has_side_effects=True, vmem_limit_bytes=56 * 1024 * 1024
        ),
        name="mixer",
    )(
        dt_raw.T,
        dt_bias.reshape(1, -1),
        a_log.reshape(1, -1),
        skip_d.reshape(1, -1),
        norm_gain.reshape(1, -1),
        b_proj,
        c_proj,
        x_in,
        multiplier_channels,
        w_out,
    )


def solution(mesh):
    return jax.shard_map(
        shards,
        mesh=mesh,
        in_specs=(
            P("seq", "grp"),
            P("seq", "grp"),
            P("seq", "grp"),
            P("seq", "grp"),
            P("seq", "grp"),
            P("grp"),
            P("grp"),
            P("grp"),
            P("grp"),
            P("grp", "seq"),
        ),
        out_specs=P("seq", "grp"),
        check_vma=False,
    )
```

time: 81.6 us -> 80.1 us (0.982)
  local copies, waits for them, and re-layouts: 3.08 us -> 1.67 us
    unnamed x4 -> x1, local copies, waits for them, and re-layouts: 3.08 us -> 1.67 us
where the time goes in v2:
time: 80.1 us; the launch traced here: 79.9 us
  Pallas kernels  78.3 us (98%)
  local copies, waits for them, and re-layouts  1.67 us (2%)
    pallas_call x1, Pallas kernels, shards(): pl.pallas_call(kernel, out_shape=jax.ShapeDtypeStruct((tokens, channels),...  78.3 us
    unnamed x1, local copies, waits for them, and re-layouts  1.67 us

profile of v2, /device:TPU:4, one launch (start us, length us, event | category | flops | bytes accessed | tf_op | source)
XLA Modules:
  0.0 79.9 jit_solution(12408913902987179917)
XLA Ops:
  0.0 78.3 %mixer.1 = bf16[128,1024]{1,0:T(8,128)(2,1)} custom-call(f32[8,128]{1,0:T(8,128)} %bitcast.5, f32[1,8]{1,0:T(1,128)} %bitcast.7, f32[1,8]{1,0:T(1,128)} %bitcast.8, f32[1,8]{1,0:T(1,128)} %bitcast.9, f32[1,1024]{1,0:T(1,128)} %bitcast.6, bf16[128,128]{1,0:T(8,128)(2,1)} %b_ref.1, bf16[128,128]{1,0:T(8,128)(2,1)} %c_ref.1, bf16[128,1024]{1,0:T(8,128)(2,1)} %x_ref.1, ...), custom_call_target="tpu_custom_call" | custom-call | tf_op jit(solution)/shard_map/mixer/pallas_call | solution.py:396
  78.3 1.7 %copy.12 = bf16[128,1024]{1,0:T(8,128)(2,1)} copy(bf16[128,1024]{1,0:T(8,128)(2,1)} %mixer.1) | data formatting | bytes 524288

commit v3 on v2

v3 whole, which is shorter than its diff:
```python
import jax
import jax.numpy as jnp
from jax import lax
from jax.experimental import pallas as pl
from jax.experimental.pallas import tpu as pltpu
from jax.sharding import PartitionSpec as P

MESH = pl.DeviceIdType.MESH
HIGH = lax.Precision.HIGHEST
WIDTH = 128
STATE = 128
NZ, NY, NX, NC = 8, 4, 4, 2
F32 = jnp.float32
BF16 = jnp.bfloat16


def split(value):
    high = value.astype(BF16)
    return high, (value - high.astype(F32)).astype(BF16)


def dot(a, b, dims=((1,), (0,))):
    return lax.dot_general(a, b, (dims, ((), ())), preferred_element_type=F32)


def kernel(
    dt_ref, bias_ref, alog_ref, skip_ref, gain_ref, b_ref, c_ref, x_ref, m_ref, w_ref,
    out_ref,
    wall, abuf, ybuf, smbuf, qbuf,
    lsend, lrecv, tsend, trecv,
    rsend, rrecv, dsend, drecv,
    esend, erecv, ssend, srecv,
    part_sums, precv, xsend, xrecv, fsend,
    w_local, w_ss, w_rs, l_ss, l_rs, t_ss, t_rs, r_ss, r_rs, d_ss, d_rs,
    e_ss, e_rs, s_ss, s_rs, a_ss, a_rs, p_ss, p_rs, x_ss, x_rs, f_ss, f_rs,
):
    seq, grp = lax.axis_index("seq"), lax.axis_index("grp")
    z, y = seq // NY, seq % NY
    x, core = grp // NC, grp % NC
    tokens, channels = x_ref.shape
    heads = channels // WIDTH
    pair = channels // NY
    cols = w_ref.shape[1]
    khalf = w_ref.shape[0] // 2
    chalf = cols // 2
    thalf = tokens // 2
    share = tokens // NC

    def device(dz=0, dy=0, dx=0, dc=0):
        return (
            ((z + dz) % NZ) * NY + (y + dy) % NY,
            ((x + dx) % NX) * NC + (core + dc) % NC,
        )

    def remote(src, dst, ss, rs, to):
        return pltpu.make_async_remote_copy(
            src_ref=src, dst_ref=dst, send_sem=ss, recv_sem=rs, device_id=to, device_id_type=MESH
        )

    sends = []

    def send(src, dst, ss, rs, to):
        copy = remote(src, dst, ss, rs, to)
        copy.start()
        sends.append(copy)

    def arrived(dst, ss, rs):
        remote(dst, dst, ss, rs, device(dz=1)).wait_recv()

    barrier = pltpu.get_barrier_semaphore()
    others = (
        [dict(dz=k) for k in range(1, NZ)]
        + [dict(dy=k) for k in range(1, NY)]
        + [dict(dx=k, dc=c) for k in range(NX) for c in range(NC) if k or c]
    )
    for other in others:
        pl.semaphore_signal(barrier, inc=1, device_id=device(**other), device_id_type=MESH)
    own_w = []
    for i in range(2):
        copy = pltpu.make_async_copy(
            w_ref.at[:, i * chalf : (i + 1) * chalf], wall.at[z, i], w_local.at[i]
        )
        copy.start()
        own_w.append(copy)

    raw = jnp.transpose(dt_ref[...]) + bias_ref[...]
    dt = jnp.maximum(raw, 0.0) + jnp.log1p(jnp.exp(-jnp.abs(raw)))
    la = -jnp.exp(alog_ref[...]) * dt
    rows = lax.broadcasted_iota(jnp.int32, (tokens, tokens), 0)
    columns = lax.broadcasted_iota(jnp.int32, (tokens, tokens), 1)
    mask = rows >= columns
    cum = lax.dot_general(
        mask.astype(F32), la, (((1,), (0,)), ((), ())), precision=HIGH, preferred_element_type=F32
    )
    total = cum[tokens - 1 : tokens, :]
    weight = jnp.exp(total - cum) * dt

    bmat, cmat = b_ref[...], c_ref[...]
    for j in range(NY):
        parts = []
        for h in range(j * heads // NY, (j + 1) * heads // NY):
            xh = x_ref[:, h * WIDTH : (h + 1) * WIDTH].astype(F32)
            parts.append(xh * weight[:, h : h + 1])
        high, low = split(jnp.concatenate(parts, axis=1))
        state = dot(bmat, high, ((0,), (0,))) + dot(bmat, low, ((0,), (0,)))
        lsend[j] = state.astype(BF16)
        tsend[j] = jnp.concatenate(
            [
                jnp.broadcast_to(total[:, h : h + 1], (8, WIDTH))
                for h in range(j * heads // NY, (j + 1) * heads // NY)
            ],
            axis=1,
        )
    logits = dot(cmat, bmat, ((1,), (1,)))
    cum_t = jnp.transpose(cum)
    dt_t = jnp.transpose(dt)
    for h in range(heads):
        span = slice(h * WIDTH, (h + 1) * WIDTH)
        decay = jnp.exp(jnp.where(mask, cum[:, h : h + 1] - cum_t[h : h + 1, :], -1e30))
        high, low = split(decay * logits * dt_t[h : h + 1, :])
        xh = x_ref[:, span]
        ybuf[:, span] = dot(high, xh) + dot(low, xh) + skip_ref[:, h : h + 1] * xh.astype(F32)
        gate = m_ref[:, span].astype(F32)
        smbuf[:, span] = gate / (1.0 + jnp.exp(-gate))

    for copy in own_w:
        copy.wait()
    pl.semaphore_wait(barrier, len(others))

    for k in range(1, NY):
        to = (y + k) % NY
        send(lsend.at[to], lrecv.at[y], l_ss.at[k - 1], l_rs.at[k - 1], device(dy=k))
        send(tsend.at[to, pl.ds(0, 1), :], trecv.at[y, pl.ds(0, 1), :], t_ss.at[k - 1], t_rs.at[k - 1], device(dy=k))
    lrecv[y] = lsend[y]
    trecv[y] = tsend[y]

    def w_part(origin, d, i):
        half = i % 2 if d == 0 else 1 - i % 2
        return wall.at[origin, i // 2, pl.ds(half * khalf, khalf), :]

    last = NZ // 2
    items = [(step, i) for step in range(last) for i in range(4)] + [(last, 0), (last, 2)]
    done = [0]

    def relay(count):
        while done[0] < count:
            step, i = items[done[0]]
            done[0] += 1
            for d, sign in enumerate((1, -1)):
                part = w_part((z - sign * step) % NZ, d, i)
                if step:
                    arrived(part, w_ss.at[d, step - 1, i], w_rs.at[d, step - 1, i])
                if step < last - 1 or (step == last - 1 and i % 2 == 0):
                    send(part, part, w_ss.at[d, step, i], w_rs.at[d, step, i], device(dz=sign))

    relay(2)

    for k in range(1, NY):
        source = (y - k) % NY
        arrived(lrecv.at[source], l_ss.at[k - 1], l_rs.at[k - 1])
        arrived(trecv.at[source, pl.ds(0, 1), :], t_ss.at[k - 1], t_rs.at[k - 1])
    before = [jnp.zeros((1, pair), F32)]
    current = lrecv[0].astype(F32)
    for j in range(NY):
        before.append(before[-1] + trecv[j][0:1, :])
        if j:
            qbuf[j - 1] = current
            current = jnp.exp(trecv[j][0:1, :]) * current + lrecv[j].astype(F32)
    size = STATE // NZ
    for k in range(NZ):
        rsend[k] = current[k * size : (k + 1) * size, :].astype(BF16)
    dsend[...] = jnp.broadcast_to(before[NY], (8, pair))
    for k in range(1, NZ):
        to = (z + k) % NZ
        send(rsend.at[to], rrecv.at[z], r_ss.at[k - 1], r_rs.at[k - 1], device(dz=k))
        send(dsend.at[pl.ds(0, 1), :], drecv.at[z, pl.ds(0, 1), :], d_ss.at[k - 1], d_rs.at[k - 1], device(dz=k))
    rrecv[z] = rsend[z]
    drecv[z] = dsend[...]
    relay(5)

    for k in range(1, NZ):
        source = (z - k) % NZ
        arrived(rrecv.at[source], r_ss.at[k - 1], r_rs.at[k - 1])
        arrived(drecv.at[source, pl.ds(0, 1), :], d_ss.at[k - 1], d_rs.at[k - 1])
    current = jnp.zeros((size, pair), F32)
    for k in range(NZ):
        esend[k] = current.astype(BF16)
        current = jnp.exp(drecv[k][0:1, :]) * current + rrecv[k].astype(F32)
    for k in range(1, NZ):
        to = (z + k) % NZ
        send(esend.at[to], erecv.at[z], e_ss.at[k - 1], e_rs.at[k - 1], device(dz=k))
    erecv[z] = esend[z]
    relay(8)
    for k in range(1, NZ):
        source = (z - k) % NZ
        arrived(erecv.at[source], e_ss.at[k - 1], e_rs.at[k - 1])
    entry = jnp.concatenate([erecv[k].astype(F32) for k in range(NZ)], axis=0)
    ssend[0] = entry.astype(BF16)
    for j in range(1, NY):
        ssend[j] = (qbuf[j - 1] + jnp.exp(before[j]) * entry).astype(BF16)
    for k in range(1, NY):
        to = (y + k) % NY
        send(ssend.at[to], srecv.at[y], s_ss.at[k - 1], s_rs.at[k - 1], device(dy=k))
    srecv[y] = ssend[y]
    relay(10)
    for k in range(1, NY):
        source = (y - k) % NY
        arrived(srecv.at[source], s_ss.at[k - 1], s_rs.at[k - 1])

    grown = jnp.exp(cum)
    squares = jnp.zeros((tokens, WIDTH), F32)
    for j in range(NY):
        inter = dot(cmat, srecv[j])
        for i in range(heads // NY):
            h = j * heads // NY + i
            span = slice(h * WIDTH, (h + 1) * WIDTH)
            value = ybuf[:, span] + grown[:, h : h + 1] * inter[:, i * WIDTH : (i + 1) * WIDTH]
            value = value * smbuf[:, span]
            ybuf[:, span] = value
            squares = squares + value * value
    mean = jnp.sum(squares, axis=1, keepdims=True) * (1.0 / channels)
    scale = lax.rsqrt(mean + 1e-05)
    abuf[0] = (ybuf[...] * scale * gain_ref[...]).astype(BF16)

    turns = (0, -1, 1, 2)

    def a_part(turn, half):
        return abuf.at[turn, pl.ds(half * thalf, thalf), :]

    for i in range(2):
        for d, sign in enumerate((1, -1)):
            half = i if d == 0 else 1 - i
            send(
                a_part(0, half),
                a_part(1 + d, half),
                a_ss.at[d, i],
                a_rs.at[d, i],
                device(dy=sign),
            )

    distances = (0, 1, -1, 2, -2, 3, -3, 4)
    stages = ((0, 1), (1, 3), (3, 4))
    whole = (0, NY)

    def owner(n):
        origin = (z + distances[n]) % NZ
        return origin // NC, origin % NC

    def partner_copy(n, span):
        rows = pl.ds(span[0], span[1] - span[0])
        index = 0 if span == whole else stages.index(span)
        return (
            part_sums.at[1 - core, n, rows],
            precv.at[n, rows],
            p_ss.at[n, index],
            p_rs.at[n, index],
        )

    def multiply(n, span):
        count = span[1] - span[0]
        origin = (z + distances[n]) % NZ
        part = jnp.concatenate([wall[origin, 0], wall[origin, 1]], axis=1)
        if span == whole:
            for first in (0, 2):
                a = abuf[first : first + 2].reshape(2 * tokens, channels)
                total = dot(a, part).reshape(2, tokens, cols)
                for c in range(NC):
                    part_sums[c, n, first : first + 2] = total[:, c * share : (c + 1) * share, :]
        else:
            a = abuf[span[0] : span[1]].reshape(count * tokens, channels)
            total = dot(a, part).reshape(count, tokens, cols)
            for c in range(NC):
                part_sums[c, n, span[0] : span[1]] = total[:, c * share : (c + 1) * share, :]
        send(*partner_copy(n, span), device(dc=1))

    def owner_copy(n, index):
        rows = pl.ds(stages[index][0], stages[index][1] - stages[index][0])
        to_x, to_core = owner(n)
        return remote(
            xsend.at[n, rows],
            xrecv.at[x, core, rows],
            x_ss.at[n, index],
            x_rs.at[x, core, index],
            (seq, to_x * NC + to_core),
        )

    def chip_sum(n, span):
        to_x, to_core = owner(n)
        own = (to_x == x) & (to_core == core)
        _, dst, ss, rs = partner_copy(n, span)
        arrived(dst, ss, rs)
        rows = slice(*span)
        both = part_sums[core, n, rows] + precv[n, rows]
        xsend[n, rows] = both.astype(BF16)

        @pl.when(own)
        def _():
            xrecv[x, core, rows] = xsend[n, rows]

        @pl.when(jnp.logical_not(own))
        def _():
            for index in range(3) if span == whole else (stages.index(span),):
                owner_copy(n, index).start()

    pending = []

    def unit(n, span):
        multiply(n, span)
        pending.append((n, span))
        if len(pending) > 1:
            chip_sum(*pending.pop(0))

    relay(11)
    for n in range(3):
        unit(n, stages[0])
    relay(12)
    for d, sign in enumerate((1, -1)):
        arrived(a_part(1 + d, d), a_ss.at[d, 0], a_rs.at[d, 0])
        send(a_part(1 + d, d), a_part(3, d), a_ss.at[d, 2], a_rs.at[d, 2], device(dy=sign))
    relay(13)
    for n in range(3, 5):
        unit(n, stages[0])
    for d in range(2):
        arrived(a_part(1 + d, 1 - d), a_ss.at[d, 1], a_rs.at[d, 1])
    for n in range(5):
        unit(n, stages[1])
    relay(15)
    for d in range(2):
        arrived(a_part(3, d), a_ss.at[d, 2], a_rs.at[d, 2])
    for n in range(5):
        unit(n, stages[2])
    relay(16)
    for n in range(5, 7):
        unit(n, whole)
    relay(18)
    unit(7, whole)
    chip_sum(*pending.pop(0))

    mine = pl.ds(pl.multiple_of(y * cols, cols), cols)
    for index in (1, 2, 0):
        span = stages[index]
        for k in range(NX):
            for c in range(NC):
                if k or c:
                    from_x, from_core = (x + k) % NX, (core + c) % NC
                    arrived(
                        xrecv.at[from_x, from_core, pl.ds(span[0], span[1] - span[0])],
                        x_ss.at[0, index],
                        x_rs.at[from_x, from_core, index],
                    )
        for t in range(*span):
            parts = []
            for c in range(NC):
                value = xrecv[0, c, t].astype(F32)
                for j in range(1, NX):
                    value = value + xrecv[j, c, t].astype(F32)
                parts.append(value.astype(BF16))
            tile = jnp.concatenate(parts, axis=0)
            if t:
                fsend[t - 1] = tile
                send(
                    fsend.at[t - 1],
                    out_ref.at[:, mine],
                    f_ss.at[t - 1],
                    f_rs.at[t - 1],
                    device(dy=turns[t]),
                )
            else:
                out_ref[:, mine] = tile
    for t in range(1, NY):
        source = (y - turns[t]) % NY
        lanes = pl.ds(pl.multiple_of(source * cols, cols), cols)
        arrived(out_ref.at[:, lanes], f_ss.at[t - 1], f_rs.at[t - 1])
    for copy in sends:
        copy.wait_send()
    for n in range(NZ):
        to_x, to_core = owner(n)

        @pl.when((to_x != x) | (to_core != core))
        def _():
            for index in range(3):
                owner_copy(n, index).wait_send()


def shards(
    x_in, multiplier_channels, b_proj, c_proj, dt_raw, dt_bias, a_log, skip_d, norm_gain, w_out
):
    tokens, channels = x_in.shape
    depth, cols = w_out.shape
    pair = channels // NY
    size = STATE // NZ
    vmem = pl.BlockSpec(memory_space=pltpu.VMEM)
    dma = pltpu.SemaphoreType.DMA
    half = cols // 2
    share = tokens // NC
    scratch = [
        pltpu.VMEM((NZ, 2, depth, half), BF16),
        pltpu.VMEM((NY, tokens, channels), BF16),
        pltpu.VMEM((tokens, channels), F32),
        pltpu.VMEM((tokens, channels), F32),
        pltpu.VMEM((NY - 1, STATE, pair), F32),
        pltpu.VMEM((NY, STATE, pair), BF16),
        pltpu.VMEM((NY, STATE, pair), BF16),
        pltpu.VMEM((NY, 8, pair), F32),
        pltpu.VMEM((NY, 8, pair), F32),
        pltpu.VMEM((NZ, size, pair), BF16),
        pltpu.VMEM((NZ, size, pair), BF16),
        pltpu.VMEM((8, pair), F32),
        pltpu.VMEM((NZ, 8, pair), F32),
        pltpu.VMEM((NZ, size, pair), BF16),
        pltpu.VMEM((NZ, size, pair), BF16),
        pltpu.VMEM((NY, STATE, pair), BF16),
        pltpu.VMEM((NY, STATE, pair), BF16),
        pltpu.VMEM((NC, NZ, NY, share, cols), F32),
        pltpu.VMEM((NZ, NY, share, cols), F32),
        pltpu.VMEM((NZ, NY, share, cols), BF16),
        pltpu.VMEM((NX, NC, NY, share, cols), BF16),
        pltpu.VMEM((NY - 1, tokens, cols), BF16),
        dma((2,)),
        dma((2, 4, 4)), dma((2, 4, 4)),
        dma((3,)), dma((3,)), dma((3,)), dma((3,)),
        dma((7,)), dma((7,)), dma((7,)), dma((7,)),
        dma((7,)), dma((7,)),
        dma((3,)), dma((3,)),
        dma((2, 3)), dma((2, 3)),
        dma((NZ, 3)), dma((NZ, 3)),
        dma((NZ, 3)), dma((NX, NC, 3)),
        dma((NY - 1,)), dma((NY - 1,)),
    ]
    return pl.pallas_call(
        kernel,
        out_shape=jax.ShapeDtypeStruct((tokens, channels), BF16),
        in_specs=[vmem] * 9 + [pl.BlockSpec(memory_space=pl.ANY)],
        out_specs=vmem,
        scratch_shapes=scratch,
        compiler_params=pltpu.CompilerParams(
            collective_id=0, has_side_effects=True, vmem_limit_bytes=56 * 1024 * 1024
        ),
        name="mixer",
    )(
        dt_raw.T,
        dt_bias.reshape(1, -1),
        a_log.reshape(1, -1),
        skip_d.reshape(1, -1),
        norm_gain.reshape(1, -1),
        b_proj,
        c_proj,
        x_in,
        multiplier_channels,
        w_out,
    )


def solution(mesh):
    return jax.shard_map(
        shards,
        mesh=mesh,
        in_specs=(
            P("seq", "grp"),
            P("seq", "grp"),
            P("seq", "grp"),
            P("seq", "grp"),
            P("seq", "grp"),
            P("grp"),
            P("grp"),
            P("grp"),
            P("grp"),
            P("grp", "seq"),
        ),
        out_specs=P("seq", "grp"),
        check_vma=False,
    )
```

time: 80.1 us -> 75.9 us (0.948)
  Pallas kernels: 78.3 us -> 74.1 us
    pallas_call x1, Pallas kernels: 78.3 us -> 74.1 us  [shards(): pl.pallas_call(kernel, out_shape=jax.ShapeDtypeStruct((tokens, channels),...]
where the time goes in v3:
time: 75.9 us; the launch traced here: 75.8 us
  Pallas kernels  74.1 us (98%)
  local copies, waits for them, and re-layouts  1.67 us (2%)
    pallas_call x1, Pallas kernels, shards(): pl.pallas_call(kernel, out_shape=jax.ShapeDtypeStruct((tokens, channels),...  74.1 us
    unnamed x1, local copies, waits for them, and re-layouts  1.67 us

profile of v3, /device:TPU:4, one launch (start us, length us, event | category | flops | bytes accessed | tf_op | source)
XLA Modules:
  0.0 75.8 jit_solution(9607384118602763324)
XLA Ops:
  0.0 74.1 %mixer.1 = bf16[128,1024]{1,0:T(8,128)(2,1)} custom-call(f32[8,128]{1,0:T(8,128)} %bitcast.5, f32[1,8]{1,0:T(1,128)} %bitcast.7, f32[1,8]{1,0:T(1,128)} %bitcast.8, f32[1,8]{1,0:T(1,128)} %bitcast.9, f32[1,1024]{1,0:T(1,128)} %bitcast.6, bf16[128,128]{1,0:T(8,128)(2,1)} %b_ref.1, bf16[128,128]{1,0:T(8,128)(2,1)} %c_ref.1, bf16[128,1024]{1,0:T(8,128)(2,1)} %x_ref.1, ...), custom_call_target="tpu_custom_call" | custom-call | tf_op jit(solution)/shard_map/mixer/pallas_call | solution.py:430
  74.1 1.7 %copy.12 = bf16[128,1024]{1,0:T(8,128)(2,1)} copy(bf16[128,1024]{1,0:T(8,128)(2,1)} %mixer.1) | data formatting | bytes 524288

commit v4 on v3

--- a/solution.py
+++ b/solution.py
@@ -24,14 +24,14 @@
 
 
 def kernel(
-    dt_ref, bias_ref, alog_ref, skip_ref, gain_ref, b_ref, c_ref, x_ref, m_ref, w_ref,
+    dt_ref, bias_ref, alog_ref, skip_ref, gain_ref, b_ref, c_ref, x_hbm, m_hbm, w_ref,
     out_ref,
-    wall, abuf, ybuf, smbuf, qbuf,
+    x_ref, m_ref, wall, abuf, ybuf, smbuf, qbuf,
     lsend, lrecv, tsend, trecv,
     rsend, rrecv, dsend, drecv,
     esend, erecv, ssend, srecv,
     part_sums, precv, xsend, xrecv, fsend,
-    w_local, w_ss, w_rs, l_ss, l_rs, t_ss, t_rs, r_ss, r_rs, d_ss, d_rs,
+    in_sems, w_local, w_ss, w_rs, l_ss, l_rs, t_ss, t_rs, r_ss, r_rs, d_ss, d_rs,
     e_ss, e_rs, s_ss, s_rs, a_ss, a_rs, p_ss, p_rs, x_ss, x_rs, f_ss, f_rs,
 ):
     seq, grp = lax.axis_index("seq"), lax.axis_index("grp")
@@ -82,6 +82,40 @@
         )
         copy.start()
         own_w.append(copy)
+    loads = [
+        pltpu.make_async_copy(x_hbm, x_ref, in_sems.at[0]),
+        pltpu.make_async_copy(m_hbm, m_ref, in_sems.at[1]),
+    ]
+    for copy in loads:
+        copy.start()
+
+    pl.semaphore_wait(barrier, len(others))
+
+    def w_part(origin, d, i):
+        half = i % 2 if d == 0 else 1 - i % 2
+        return wall.at[origin, i // 2, pl.ds(half * khalf, khalf), :]
+
+    last = NZ // 2
+    items = [(step, i) for step in range(last) for i in range(4)] + [(last, 0), (last, 2)]
+    done = [0]
+
+    def relay(count):
+        while done[0] < count:
+            step, i = items[done[0]]
+            done[0] += 1
+            for d, sign in enumerate((1, -1)):
+                part = source = w_part((z - sign * step) % NZ, d, i)
+                if not step:
+                    half = i % 2 if d == 0 else 1 - i % 2
+                    source = w_ref.at[
+                        pl.ds(half * khalf, khalf), pl.ds(i // 2 * chalf, chalf)
+                    ]
+                else:
+                    arrived(part, w_ss.at[d, step - 1, i], w_rs.at[d, step - 1, i])
+                if step < last - 1 or (step == last - 1 and i % 2 == 0):
+                    send(source, part, w_ss.at[d, step, i], w_rs.at[d, step, i], device(dz=sign))
+
+    relay(3)
 
     raw = jnp.transpose(dt_ref[...]) + bias_ref[...]
     dt = jnp.maximum(raw, 0.0) + jnp.log1p(jnp.exp(-jnp.abs(raw)))
@@ -95,6 +129,8 @@
     total = cum[tokens - 1 : tokens, :]
     weight = jnp.exp(total - cum) * dt
 
+    for copy in loads + own_w:
+        copy.wait()
     bmat, cmat = b_ref[...], c_ref[...]
     for j in range(NY):
         parts = []
@@ -123,37 +159,12 @@
         gate = m_ref[:, span].astype(F32)
         smbuf[:, span] = gate / (1.0 + jnp.exp(-gate))
 
-    for copy in own_w:
-        copy.wait()
-    pl.semaphore_wait(barrier, len(others))
-
     for k in range(1, NY):
         to = (y + k) % NY
         send(lsend.at[to], lrecv.at[y], l_ss.at[k - 1], l_rs.at[k - 1], device(dy=k))
         send(tsend.at[to, pl.ds(0, 1), :], trecv.at[y, pl.ds(0, 1), :], t_ss.at[k - 1], t_rs.at[k - 1], device(dy=k))
     lrecv[y] = lsend[y]
     trecv[y] = tsend[y]
-
-    def w_part(origin, d, i):
-        half = i % 2 if d == 0 else 1 - i % 2
-        return wall.at[origin, i // 2, pl.ds(half * khalf, khalf), :]
-
-    last = NZ // 2
-    items = [(step, i) for step in range(last) for i in range(4)] + [(last, 0), (last, 2)]
-    done = [0]
-
-    def relay(count):
-        while done[0] < count:
-            step, i = items[done[0]]
-            done[0] += 1
-            for d, sign in enumerate((1, -1)):
-                part = w_part((z - sign * step) % NZ, d, i)
-                if step:
-                    arrived(part, w_ss.at[d, step - 1, i], w_rs.at[d, step - 1, i])
-                if step < last - 1 or (step == last - 1 and i % 2 == 0):
-                    send(part, part, w_ss.at[d, step, i], w_rs.at[d, step, i], device(dz=sign))
-
-    relay(2)
 
     for k in range(1, NY):
         source = (y - k) % NY
@@ -246,67 +257,75 @@
         origin = (z + distances[n]) % NZ
         return origin // NC, origin % NC
 
-    def partner_copy(n, span):
+    def lanes_of(half):
+        return pl.ds(0, cols) if half is None else pl.ds(half * chalf, chalf)
+
+    def index_of(span, half):
+        return (half or 0) if span == whole else stages.index(span)
+
+    def partner_copy(n, span, half):
         rows = pl.ds(span[0], span[1] - span[0])
-        index = 0 if span == whole else stages.index(span)
+        index = index_of(span, half)
         return (
-            part_sums.at[1 - core, n, rows],
-            precv.at[n, rows],
+            part_sums.at[1 - core, n, rows, :, lanes_of(half)],
+            precv.at[n, rows, :, lanes_of(half)],
             p_ss.at[n, index],
             p_rs.at[n, index],
         )
 
-    def multiply(n, span):
-        count = span[1] - span[0]
+    def multiply(n, span, half):
         origin = (z + distances[n]) % NZ
-        part = jnp.concatenate([wall[origin, 0], wall[origin, 1]], axis=1)
-        if span == whole:
-            for first in (0, 2):
-                a = abuf[first : first + 2].reshape(2 * tokens, channels)
-                total = dot(a, part).reshape(2, tokens, cols)
-                for c in range(NC):
-                    part_sums[c, n, first : first + 2] = total[:, c * share : (c + 1) * share, :]
+        if half is None:
+            part = jnp.concatenate([wall[origin, 0], wall[origin, 1]], axis=1)
         else:
-            a = abuf[span[0] : span[1]].reshape(count * tokens, channels)
-            total = dot(a, part).reshape(count, tokens, cols)
+            part = wall[origin, half]
+        width = part.shape[1]
+        step = min(2, span[1] - span[0])
+        for first in range(span[0], span[1], step):
+            a = abuf[first : first + step].reshape(step * tokens, channels)
+            total = dot(a, part).reshape(step, tokens, width)
             for c in range(NC):
-                part_sums[c, n, span[0] : span[1]] = total[:, c * share : (c + 1) * share, :]
-        send(*partner_copy(n, span), device(dc=1))
-
-    def owner_copy(n, index):
-        rows = pl.ds(stages[index][0], stages[index][1] - stages[index][0])
+                part_sums[c, n, first : first + step, :, lanes_of(half)] = total[
+                    :, c * share : (c + 1) * share, :
+                ]
+        send(*partner_copy(n, span, half), device(dc=1))
+
+    def owner_copy(n, span, half):
+        rows = pl.ds(span[0], span[1] - span[0])
         to_x, to_core = owner(n)
         return remote(
-            xsend.at[n, rows],
-            xrecv.at[x, core, rows],
-            x_ss.at[n, index],
-            x_rs.at[x, core, index],
+            xsend.at[n, rows, :, lanes_of(half)],
+            xrecv.at[x, core, rows, :, lanes_of(half)],
+            x_ss.at[n, index_of(span, half)],
+            x_rs.at[x, core],
             (seq, to_x * NC + to_core),
         )
 
-    def chip_sum(n, span):
+    def chip_sum(n, span, half):
         to_x, to_core = owner(n)
         own = (to_x == x) & (to_core == core)
-        _, dst, ss, rs = partner_copy(n, span)
+        _, dst, ss, rs = partner_copy(n, span, half)
         arrived(dst, ss, rs)
-        rows = slice(*span)
-        both = part_sums[core, n, rows] + precv[n, rows]
-        xsend[n, rows] = both.astype(BF16)
+        at = (slice(*span), slice(None), lanes_of(half))
+        both = part_sums[(core, n) + at] + precv[(n,) + at]
+        xsend[(n,) + at] = both.astype(BF16)
 
         @pl.when(own)
         def _():
-            xrecv[x, core, rows] = xsend[n, rows]
+            xrecv[(x, core) + at] = xsend[(n,) + at]
 
         @pl.when(jnp.logical_not(own))
         def _():
-            for index in range(3) if span == whole else (stages.index(span),):
-                owner_copy(n, index).start()
+            owner_copy(n, span, half).start()
 
     pending = []
 
-    def unit(n, span):
-        multiply(n, span)
-        pending.append((n, span))
+    units = []
+
+    def unit(n, span, half=None):
+        multiply(n, span, half)
+        units.append((n, span, half))
+        pending.append((n, span, half))
         if len(pending) > 1:
             chip_sum(*pending.pop(0))
 
@@ -332,41 +351,37 @@
     relay(16)
     for n in range(5, 7):
         unit(n, whole)
+    relay(17)
+    unit(7, whole, 0)
     relay(18)
-    unit(7, whole)
+    unit(7, whole, 1)
     chip_sum(*pending.pop(0))
 
     mine = pl.ds(pl.multiple_of(y * cols, cols), cols)
-    for index in (1, 2, 0):
-        span = stages[index]
-        for k in range(NX):
-            for c in range(NC):
-                if k or c:
-                    from_x, from_core = (x + k) % NX, (core + c) % NC
-                    arrived(
-                        xrecv.at[from_x, from_core, pl.ds(span[0], span[1] - span[0])],
-                        x_ss.at[0, index],
-                        x_rs.at[from_x, from_core, index],
-                    )
-        for t in range(*span):
-            parts = []
-            for c in range(NC):
-                value = xrecv[0, c, t].astype(F32)
-                for j in range(1, NX):
-                    value = value + xrecv[j, c, t].astype(F32)
-                parts.append(value.astype(BF16))
-            tile = jnp.concatenate(parts, axis=0)
-            if t:
-                fsend[t - 1] = tile
-                send(
-                    fsend.at[t - 1],
-                    out_ref.at[:, mine],
-                    f_ss.at[t - 1],
-                    f_rs.at[t - 1],
-                    device(dy=turns[t]),
-                )
-            else:
-                out_ref[:, mine] = tile
+    for k in range(NX):
+        for c in range(NC):
+            if k or c:
+                from_x, from_core = (x + k) % NX, (core + c) % NC
+                arrived(xrecv.at[from_x, from_core], x_ss.at[0, 0], x_rs.at[from_x, from_core])
+    for t in (3, 1, 2, 0):
+        parts = []
+        for c in range(NC):
+            value = xrecv[0, c, t].astype(F32)
+            for j in range(1, NX):
+                value = value + xrecv[j, c, t].astype(F32)
+            parts.append(value.astype(BF16))
+        tile = jnp.concatenate(parts, axis=0)
+        if t:
+            fsend[t - 1] = tile
+            send(
+                fsend.at[t - 1],
+                out_ref.at[:, mine],
+                f_ss.at[t - 1],
+                f_rs.at[t - 1],
+                device(dy=turns[t]),
+            )
+        else:
+            out_ref[:, mine] = tile
     for t in range(1, NY):
         source = (y - turns[t]) % NY
         lanes = pl.ds(pl.multiple_of(source * cols, cols), cols)
@@ -378,8 +393,9 @@
 
         @pl.when((to_x != x) | (to_core != core))
         def _():
-            for index in range(3):
-                owner_copy(n, index).wait_send()
+            for other in units:
+                if other[0] == n:
+                    owner_copy(*other).wait_send()
 
 
 def shards(
@@ -394,6 +410,8 @@
     half = cols // 2
     share = tokens // NC
     scratch = [
+        pltpu.VMEM((tokens, channels), BF16),
+        pltpu.VMEM((tokens, channels), BF16),
         pltpu.VMEM((NZ, 2, depth, half), BF16),
         pltpu.VMEM((NY, tokens, channels), BF16),
         pltpu.VMEM((tokens, channels), F32),
@@ -417,6 +435,7 @@
         pltpu.VMEM((NX, NC, NY, share, cols), BF16),
         pltpu.VMEM((NY - 1, tokens, cols), BF16),
         dma((2,)),
+        dma((2,)),
         dma((2, 4, 4)), dma((2, 4, 4)),
         dma((3,)), dma((3,)), dma((3,)), dma((3,)),
         dma((7,)), dma((7,)), dma((7,)), dma((7,)),
@@ -424,13 +443,13 @@
         dma((3,)), dma((3,)),
         dma((2, 3)), dma((2, 3)),
         dma((NZ, 3)), dma((NZ, 3)),
-        dma((NZ, 3)), dma((NX, NC, 3)),
+        dma((NZ, 3)), dma((NX, NC)),
         dma((NY - 1,)), dma((NY - 1,)),
     ]
     return pl.pallas_call(
         kernel,
-        out_shape=jax.ShapeDtypeStruct((tokens, channels), BF16),
-        in_specs=[vmem] * 9 + [pl.BlockSpec(memory_space=pl.ANY)],
+        out_shape=pltpu.VMEM((tokens, channels), BF16),
+        in_specs=[vmem] * 7 + [pl.BlockSpec(memory_space=pl.ANY)] * 3,
         out_specs=vmem,
         scratch_shapes=scratch,
         compiler_params=pltpu.CompilerParams(

time: 75.9 us -> 72 us (0.949)
  Pallas kernels: 74.1 us -> 71.1 us
  local copies, waits for them, and re-layouts: 1.67 us -> 0.71 us
    pallas_call x1, Pallas kernels: 74.1 us -> 71.1 us  [shards(): pl.pallas_call(kernel, out_shape=pltpu.VMEM((tokens, channels), BF16), in...]
    unnamed x1, local copies, waits for them, and re-layouts: 1.67 us -> 0.71 us
where the time goes in v4:
time: 72 us; the launch traced here: 71.8 us
  Pallas kernels  71.1 us (99%)
    pallas_call x1, Pallas kernels, shards(): pl.pallas_call(kernel, out_shape=pltpu.VMEM((tokens, channels), BF16), in...  71.1 us

profile of v4, /device:TPU:4, one launch (start us, length us, event | category | flops | bytes accessed | tf_op | source)
XLA Modules:
  0.0 71.8 jit_solution(9568162763966705567)
XLA Ops:
  0.0 71.1 %mixer.1 = bf16[128,1024]{1,0:T(8,128)(2,1)S(1)} custom-call(f32[8,128]{1,0:T(8,128)} %bitcast.5, f32[1,8]{1,0:T(1,128)} %bitcast.7, f32[1,8]{1,0:T(1,128)} %bitcast.8, f32[1,8]{1,0:T(1,128)} %bitcast.9, f32[1,1024]{1,0:T(1,128)} %bitcast.6, bf16[128,128]{1,0:T(8,128)(2,1)} %b_ref.1, bf16[128,128]{1,0:T(8,128)(2,1)} %c_ref.1, bf16[128,1024]{1,0:T(8,128)(2,1)} %x_hbm.1, ...), custom_call_target="tpu_custom_call" | custom-call | tf_op jit(solution)/shard_map/mixer/pallas_call | solution.py:449
  71.1 0.7 copy.12

commit v5 on v4

--- a/solution.py
+++ b/solution.py
@@ -32,7 +32,7 @@
     esend, erecv, ssend, srecv,
     part_sums, precv, xsend, xrecv, fsend,
     in_sems, w_local, w_ss, w_rs, l_ss, l_rs, t_ss, t_rs, r_ss, r_rs, d_ss, d_rs,
-    e_ss, e_rs, s_ss, s_rs, a_ss, a_rs, p_ss, p_rs, x_ss, x_rs, f_ss, f_rs,
+    e_ss, e_rs, s_ss, s_rs, a_ss, a_rs, p_ss, p_rs, x_ss, x_rs, f_ss, o_ss, f_rs,
 ):
     seq, grp = lax.axis_index("seq"), lax.axis_index("grp")
     z, y = seq // NY, seq % NY
@@ -57,15 +57,14 @@
             src_ref=src, dst_ref=dst, send_sem=ss, recv_sem=rs, device_id=to, device_id_type=MESH
         )
 
-    sends = []
-
     def send(src, dst, ss, rs, to):
-        copy = remote(src, dst, ss, rs, to)
-        copy.start()
-        sends.append(copy)
-
-    def arrived(dst, ss, rs):
-        remote(dst, dst, ss, rs, device(dz=1)).wait_recv()
+        remote(src, dst, ss, rs, to).start()
+
+    def sent(like, ss):
+        remote(like, like, ss, f_rs, device(dz=1)).wait_send()
+
+    def arrived(like, rs):
+        remote(like, like, w_ss, rs, device(dz=1)).wait_recv()
 
     barrier = pltpu.get_barrier_semaphore()
     others = (
@@ -111,9 +110,9 @@
                         pl.ds(half * khalf, khalf), pl.ds(i // 2 * chalf, chalf)
                     ]
                 else:
-                    arrived(part, w_ss.at[d, step - 1, i], w_rs.at[d, step - 1, i])
+                    arrived(part, w_rs.at[d, step - 1, i])
                 if step < last - 1 or (step == last - 1 and i % 2 == 0):
-                    send(source, part, w_ss.at[d, step, i], w_rs.at[d, step, i], device(dz=sign))
+                    send(source, part, w_ss, w_rs.at[d, step, i], device(dz=sign))
 
     relay(3)
 
@@ -161,15 +160,13 @@
 
     for k in range(1, NY):
         to = (y + k) % NY
-        send(lsend.at[to], lrecv.at[y], l_ss.at[k - 1], l_rs.at[k - 1], device(dy=k))
-        send(tsend.at[to, pl.ds(0, 1), :], trecv.at[y, pl.ds(0, 1), :], t_ss.at[k - 1], t_rs.at[k - 1], device(dy=k))
+        send(lsend.at[to], lrecv.at[y], l_ss, l_rs, device(dy=k))
+        send(tsend.at[to, pl.ds(0, 1), :], trecv.at[y, pl.ds(0, 1), :], t_ss, t_rs, device(dy=k))
     lrecv[y] = lsend[y]
     trecv[y] = tsend[y]
 
-    for k in range(1, NY):
-        source = (y - k) % NY
-        arrived(lrecv.at[source], l_ss.at[k - 1], l_rs.at[k - 1])
-        arrived(trecv.at[source, pl.ds(0, 1), :], t_ss.at[k - 1], t_rs.at[k - 1])
+    arrived(lrecv.at[pl.ds(0, NY - 1)], l_rs)
+    arrived(trecv.at[pl.ds(0, NY - 1), pl.ds(0, 1), :], t_rs)
     before = [jnp.zeros((1, pair), F32)]
     current = lrecv[0].astype(F32)
     for j in range(NY):
@@ -183,40 +180,34 @@
     dsend[...] = jnp.broadcast_to(before[NY], (8, pair))
     for k in range(1, NZ):
         to = (z + k) % NZ
-        send(rsend.at[to], rrecv.at[z], r_ss.at[k - 1], r_rs.at[k - 1], device(dz=k))
-        send(dsend.at[pl.ds(0, 1), :], drecv.at[z, pl.ds(0, 1), :], d_ss.at[k - 1], d_rs.at[k - 1], device(dz=k))
+        send(rsend.at[to], rrecv.at[z], r_ss, r_rs, device(dz=k))
+        send(dsend.at[pl.ds(0, 1), :], drecv.at[z, pl.ds(0, 1), :], d_ss, d_rs, device(dz=k))
     rrecv[z] = rsend[z]
     drecv[z] = dsend[...]
     relay(5)
 
-    for k in range(1, NZ):
-        source = (z - k) % NZ
-        arrived(rrecv.at[source], r_ss.at[k - 1], r_rs.at[k - 1])
-        arrived(drecv.at[source, pl.ds(0, 1), :], d_ss.at[k - 1], d_rs.at[k - 1])
+    arrived(rrecv.at[pl.ds(0, NZ - 1)], r_rs)
+    arrived(drecv.at[pl.ds(0, NZ - 1), pl.ds(0, 1), :], d_rs)
     current = jnp.zeros((size, pair), F32)
     for k in range(NZ):
         esend[k] = current.astype(BF16)
         current = jnp.exp(drecv[k][0:1, :]) * current + rrecv[k].astype(F32)
     for k in range(1, NZ):
         to = (z + k) % NZ
-        send(esend.at[to], erecv.at[z], e_ss.at[k - 1], e_rs.at[k - 1], device(dz=k))
+        send(esend.at[to], erecv.at[z], e_ss, e_rs, device(dz=k))
     erecv[z] = esend[z]
     relay(8)
-    for k in range(1, NZ):
-        source = (z - k) % NZ
-        arrived(erecv.at[source], e_ss.at[k - 1], e_rs.at[k - 1])
+    arrived(erecv.at[pl.ds(0, NZ - 1)], e_rs)
     entry = jnp.concatenate([erecv[k].astype(F32) for k in range(NZ)], axis=0)
     ssend[0] = entry.astype(BF16)
     for j in range(1, NY):
         ssend[j] = (qbuf[j - 1] + jnp.exp(before[j]) * entry).astype(BF16)
     for k in range(1, NY):
         to = (y + k) % NY
-        send(ssend.at[to], srecv.at[y], s_ss.at[k - 1], s_rs.at[k - 1], device(dy=k))
+        send(ssend.at[to], srecv.at[y], s_ss, s_rs, device(dy=k))
     srecv[y] = ssend[y]
     relay(10)
-    for k in range(1, NY):
-        source = (y - k) % NY
-        arrived(srecv.at[source], s_ss.at[k - 1], s_rs.at[k - 1])
+    arrived(srecv.at[pl.ds(0, NY - 1)], s_rs)
 
     grown = jnp.exp(cum)
     squares = jnp.zeros((tokens, WIDTH), F32)
@@ -244,7 +235,7 @@
             send(
                 a_part(0, half),
                 a_part(1 + d, half),
-                a_ss.at[d, i],
+                a_ss,
                 a_rs.at[d, i],
                 device(dy=sign),
             )
@@ -269,7 +260,7 @@
         return (
             part_sums.at[1 - core, n, rows, :, lanes_of(half)],
             precv.at[n, rows, :, lanes_of(half)],
-            p_ss.at[n, index],
+            p_ss,
             p_rs.at[n, index],
         )
 
@@ -290,41 +281,55 @@
                 ]
         send(*partner_copy(n, span, half), device(dc=1))
 
-    def owner_copy(n, span, half):
+    slab = share // NX
+
+    def chip_sum(n, span, half):
+        _, dst, _, rs = partner_copy(n, span, half)
+        arrived(dst, rs)
+        lanes = lanes_of(half)
+        both = part_sums[core, n, span[0] : span[1], :, lanes]
+        both = (both + precv[n, span[0] : span[1], :, lanes]).astype(BF16)
+        for j in range(NX):
+            xsend[n, j, span[0] : span[1], :, lanes] = both[:, j * slab : (j + 1) * slab, :]
         rows = pl.ds(span[0], span[1] - span[0])
+        for k in range(1, NX):
+            send(
+                xsend.at[n, (x + k) % NX, rows, :, lanes],
+                xrecv.at[n, k - 1, rows, :, lanes],
+                x_ss,
+                x_rs.at[n],
+                device(dx=k),
+            )
+
+    mine = pl.ds(pl.multiple_of(y * cols, cols), cols)
+    place = pl.ds(pl.multiple_of(core * share + x * slab, slab), slab)
+
+    def finish(n):
+        value = xsend[n, x].astype(F32)
+        arrived(xrecv.at[n], x_rs.at[n])
+        for k in range(1, NX):
+            value = value + xrecv[n, k - 1].astype(F32)
+        fsend[n] = value.astype(BF16)
         to_x, to_core = owner(n)
-        return remote(
-            xsend.at[n, rows, :, lanes_of(half)],
-            xrecv.at[x, core, rows, :, lanes_of(half)],
-            x_ss.at[n, index_of(span, half)],
-            x_rs.at[x, core],
-            (seq, to_x * NC + to_core),
-        )
-
-    def chip_sum(n, span, half):
-        to_x, to_core = owner(n)
+        for t in (3, 1, 2):
+            to = (z * NY + (y + turns[t]) % NY, to_x * NC + to_core)
+            send(fsend.at[n, t], out_ref.at[place, mine], f_ss, f_rs, to)
         own = (to_x == x) & (to_core == core)
-        _, dst, ss, rs = partner_copy(n, span, half)
-        arrived(dst, ss, rs)
-        at = (slice(*span), slice(None), lanes_of(half))
-        both = part_sums[(core, n) + at] + precv[(n,) + at]
-        xsend[(n,) + at] = both.astype(BF16)
 
         @pl.when(own)
         def _():
-            xrecv[(x, core) + at] = xsend[(n,) + at]
+            pltpu.make_async_copy(fsend.at[n, 0], out_ref.at[place, mine], f_rs).start()
 
         @pl.when(jnp.logical_not(own))
         def _():
-            owner_copy(n, span, half).start()
+            send(
+                fsend.at[n, 0], out_ref.at[place, mine], o_ss, f_rs, (seq, to_x * NC + to_core)
+            )
 
     pending = []
-
-    units = []
 
     def unit(n, span, half=None):
         multiply(n, span, half)
-        units.append((n, span, half))
         pending.append((n, span, half))
         if len(pending) > 1:
             chip_sum(*pending.pop(0))
@@ -334,68 +339,45 @@
         unit(n, stages[0])
     relay(12)
     for d, sign in enumerate((1, -1)):
-        arrived(a_part(1 + d, d), a_ss.at[d, 0], a_rs.at[d, 0])
-        send(a_part(1 + d, d), a_part(3, d), a_ss.at[d, 2], a_rs.at[d, 2], device(dy=sign))
+        arrived(a_part(1 + d, d), a_rs.at[d, 0])
+        send(a_part(1 + d, d), a_part(3, d), a_ss, a_rs.at[d, 2], device(dy=sign))
     relay(13)
     for n in range(3, 5):
         unit(n, stages[0])
     for d in range(2):
-        arrived(a_part(1 + d, 1 - d), a_ss.at[d, 1], a_rs.at[d, 1])
+        arrived(a_part(1 + d, 1 - d), a_rs.at[d, 1])
     for n in range(5):
         unit(n, stages[1])
     relay(15)
+    sent(lsend.at[pl.ds(0, NY - 1)], l_ss)
+    sent(tsend.at[pl.ds(0, NY - 1), pl.ds(0, 1), :], t_ss)
+    sent(rsend.at[pl.ds(0, NZ - 1)], r_ss)
+    sent(drecv.at[pl.ds(0, NZ - 1), pl.ds(0, 1), :], d_ss)
+    sent(esend.at[pl.ds(0, NZ - 1)], e_ss)
+    sent(ssend.at[pl.ds(0, NY - 1)], s_ss)
     for d in range(2):
-        arrived(a_part(3, d), a_ss.at[d, 2], a_rs.at[d, 2])
+        arrived(a_part(3, d), a_rs.at[d, 2])
     for n in range(5):
         unit(n, stages[2])
     relay(16)
-    for n in range(5, 7):
-        unit(n, whole)
+    unit(5, whole)
+    unit(6, whole)
+    sent(abuf.at[pl.ds(0, 3)], a_ss)
     relay(17)
     unit(7, whole, 0)
     relay(18)
     unit(7, whole, 1)
     chip_sum(*pending.pop(0))
-
-    mine = pl.ds(pl.multiple_of(y * cols, cols), cols)
-    for k in range(NX):
-        for c in range(NC):
-            if k or c:
-                from_x, from_core = (x + k) % NX, (core + c) % NC
-                arrived(xrecv.at[from_x, from_core], x_ss.at[0, 0], x_rs.at[from_x, from_core])
-    for t in (3, 1, 2, 0):
-        parts = []
-        for c in range(NC):
-            value = xrecv[0, c, t].astype(F32)
-            for j in range(1, NX):
-                value = value + xrecv[j, c, t].astype(F32)
-            parts.append(value.astype(BF16))
-        tile = jnp.concatenate(parts, axis=0)
-        if t:
-            fsend[t - 1] = tile
-            send(
-                fsend.at[t - 1],
-                out_ref.at[:, mine],
-                f_ss.at[t - 1],
-                f_rs.at[t - 1],
-                device(dy=turns[t]),
-            )
-        else:
-            out_ref[:, mine] = tile
-    for t in range(1, NY):
-        source = (y - turns[t]) % NY
-        lanes = pl.ds(pl.multiple_of(source * cols, cols), cols)
-        arrived(out_ref.at[:, lanes], f_ss.at[t - 1], f_rs.at[t - 1])
-    for copy in sends:
-        copy.wait_send()
-    for n in range(NZ):
-        to_x, to_core = owner(n)
-
-        @pl.when((to_x != x) | (to_core != core))
-        def _():
-            for other in units:
-                if other[0] == n:
-                    owner_copy(*other).wait_send()
+    for n in range(NZ - 1):
+        finish(n)
+    finish(NZ - 1)
+
+    sent(wall.at[pl.ds(0, NZ - 1)], w_ss)
+    sent(precv, p_ss)
+    sent(xrecv, x_ss)
+    arrived(out_ref, f_rs)
+    sent(fsend.at[:, pl.ds(1, NY - 1)], f_ss)
+    sent(fsend.at[pl.ds(0, NZ - 1), 0], o_ss)
 
 
 def shards(
@@ -431,20 +413,20 @@
         pltpu.VMEM((NY, STATE, pair), BF16),
         pltpu.VMEM((NC, NZ, NY, share, cols), F32),
         pltpu.VMEM((NZ, NY, share, cols), F32),
-        pltpu.VMEM((NZ, NY, share, cols), BF16),
-        pltpu.VMEM((NX, NC, NY, share, cols), BF16),
-        pltpu.VMEM((NY - 1, tokens, cols), BF16),
+        pltpu.VMEM((NZ, NX, NY, share // NX, cols), BF16),
+        pltpu.VMEM((NZ, NX - 1, NY, share // NX, cols), BF16),
+        pltpu.VMEM((NZ, NY, share // NX, cols), BF16),
         dma((2,)),
         dma((2,)),
-        dma((2, 4, 4)), dma((2, 4, 4)),
-        dma((3,)), dma((3,)), dma((3,)), dma((3,)),
-        dma((7,)), dma((7,)), dma((7,)), dma((7,)),
-        dma((7,)), dma((7,)),
-        dma((3,)), dma((3,)),
-        dma((2, 3)), dma((2, 3)),
-        dma((NZ, 3)), dma((NZ, 3)),
-        dma((NZ, 3)), dma((NX, NC)),
-        dma((NY - 1,)), dma((NY - 1,)),
+        dma, dma((2, 4, 4)),
+        dma, dma, dma, dma,
+        dma, dma, dma, dma,
+        dma, dma,
+        dma, dma,
+        dma, dma((2, 3)),
+        dma, dma((NZ, 3)),
+        dma, dma((NZ,)),
+        dma, dma, dma,
     ]
     return pl.pallas_call(
         kernel,

time: 72 us -> 65.9 us (0.915)
  the two profiles are of different devices: /device:TPU:4 before, /device:TPU:1 now
where the time goes in v5:
time: 65.9 us; the launch traced here: 65.8 us
  Pallas kernels  65.1 us (99%)
  local copies, waits for them, and re-layouts  0.71 us (1%)
    pallas_call x1, Pallas kernels, shards(): pl.pallas_call(kernel, out_shape=pltpu.VMEM((tokens, channels), BF16), in...  65.1 us

profile of v5, /device:TPU:1, one launch (start us, length us, event | category | flops | bytes accessed | tf_op | source)
XLA Modules:
  0.0 65.8 jit_solution(14221646406491036096)
XLA Ops:
  0.0 65.1 %mixer.1 = bf16[128,1024]{1,0:T(8,128)(2,1)S(1)} custom-call(f32[8,128]{1,0:T(8,128)} %bitcast.5, f32[1,8]{1,0:T(1,128)} %bitcast.7, f32[1,8]{1,0:T(1,128)} %bitcast.8, f32[1,8]{1,0:T(1,128)} %bitcast.9, f32[1,1024]{1,0:T(1,128)} %bitcast.6, bf16[128,128]{1,0:T(8,128)(2,1)} %b_ref.1, bf16[128,128]{1,0:T(8,128)(2,1)} %c_ref.1, bf16[128,1024]{1,0:T(8,128)(2,1)} %x_hbm.1, ...), custom_call_target="tpu_custom_call" | custom-call | tf_op jit(solution)/shard_map/mixer/pallas_call | solution.py:431
  65.1 0.7 %copy.12 = bf16[128,1024]{1,0:T(8,128)(2,1)} copy(bf16[128,1024]{1,0:T(8,128)(2,1)S(1)} %mixer.1) | data formatting | bytes 524288

commit v6 on v5

--- a/solution.py
+++ b/solution.py
@@ -24,9 +24,9 @@
 
 
 def kernel(
-    dt_ref, bias_ref, alog_ref, skip_ref, gain_ref, b_ref, c_ref, x_hbm, m_hbm, w_ref,
+    dt_hbm, bias_hbm, alog_hbm, skip_hbm, gain_hbm, b_hbm, c_hbm, x_hbm, m_hbm, w_ref,
     out_ref,
-    x_ref, m_ref, wall, abuf, ybuf, smbuf, qbuf,
+    dt_ref, bias_ref, alog_ref, skip_ref, gain_ref, b_ref, c_ref, x_ref, m_ref, wall, abuf, ybuf, smbuf, qbuf,
     lsend, lrecv, tsend, trecv,
     rsend, rrecv, dsend, drecv,
     esend, erecv, ssend, srecv,
@@ -82,8 +82,20 @@
         copy.start()
         own_w.append(copy)
     loads = [
-        pltpu.make_async_copy(x_hbm, x_ref, in_sems.at[0]),
-        pltpu.make_async_copy(m_hbm, m_ref, in_sems.at[1]),
+        pltpu.make_async_copy(src, dst, in_sems.at[i])
+        for i, (src, dst) in enumerate(
+            (
+                (dt_hbm, dt_ref),
+                (bias_hbm, bias_ref),
+                (alog_hbm, alog_ref),
+                (x_hbm, x_ref),
+                (b_hbm, b_ref),
+                (c_hbm, c_ref),
+                (skip_hbm, skip_ref),
+                (m_hbm, m_ref),
+                (gain_hbm, gain_ref),
+            )
+        )
     ]
     for copy in loads:
         copy.start()
@@ -116,6 +128,8 @@
 
     relay(3)
 
+    for copy in loads + own_w:
+        copy.wait()
     raw = jnp.transpose(dt_ref[...]) + bias_ref[...]
     dt = jnp.maximum(raw, 0.0) + jnp.log1p(jnp.exp(-jnp.abs(raw)))
     la = -jnp.exp(alog_ref[...]) * dt
@@ -128,8 +142,6 @@
     total = cum[tokens - 1 : tokens, :]
     weight = jnp.exp(total - cum) * dt
 
-    for copy in loads + own_w:
-        copy.wait()
     bmat, cmat = b_ref[...], c_ref[...]
     for j in range(NY):
         parts = []
@@ -206,7 +218,7 @@
         to = (y + k) % NY
         send(ssend.at[to], srecv.at[y], s_ss, s_rs, device(dy=k))
     srecv[y] = ssend[y]
-    relay(10)
+    relay(11)
     arrived(srecv.at[pl.ds(0, NY - 1)], s_rs)
 
     grown = jnp.exp(cum)
@@ -391,7 +403,15 @@
     dma = pltpu.SemaphoreType.DMA
     half = cols // 2
     share = tokens // NC
+    heads = channels // WIDTH
     scratch = [
+        pltpu.VMEM((heads, tokens), F32),
+        pltpu.VMEM((1, heads), F32),
+        pltpu.VMEM((1, heads), F32),
+        pltpu.VMEM((1, heads), F32),
+        pltpu.VMEM((1, channels), F32),
+        pltpu.VMEM((tokens, STATE), BF16),
+        pltpu.VMEM((tokens, STATE), BF16),
         pltpu.VMEM((tokens, channels), BF16),
         pltpu.VMEM((tokens, channels), BF16),
         pltpu.VMEM((NZ, 2, depth, half), BF16),
@@ -416,7 +436,7 @@
         pltpu.VMEM((NZ, NX, NY, share // NX, cols), BF16),
         pltpu.VMEM((NZ, NX - 1, NY, share // NX, cols), BF16),
         pltpu.VMEM((NZ, NY, share // NX, cols), BF16),
-        dma((2,)),
+        dma((9,)),
         dma((2,)),
         dma, dma((2, 4, 4)),
         dma, dma, dma, dma,
@@ -431,7 +451,7 @@
     return pl.pallas_call(
         kernel,
         out_shape=pltpu.VMEM((tokens, channels), BF16),
-        in_specs=[vmem] * 7 + [pl.BlockSpec(memory_space=pl.ANY)] * 3,
+        in_specs=[pl.BlockSpec(memory_space=pl.ANY)] * 10,
         out_specs=vmem,
         scratch_shapes=scratch,
         compiler_params=pltpu.CompilerParams(

time: 65.9 us -> 64.6 us (0.980)
  the two profiles are of different devices: /device:TPU:1 before, /device:TPU:4 now
where the time goes in v6:
time: 64.6 us; the launch traced here: 63.6 us
  Pallas kernels  62.9 us (97%)
  local copies, waits for them, and re-layouts  0.71 us (1%)
    pallas_call x1, Pallas kernels, shards(): pl.pallas_call(kernel, out_shape=pltpu.VMEM((tokens, channels), BF16), in...  62.9 us

profile of v6, /device:TPU:4, one launch (start us, length us, event | category | flops | bytes accessed | tf_op | source)
XLA Modules:
  0.0 63.6 jit_solution(15719532336497636236)
XLA Ops:
  0.0 62.9 %mixer.1 = bf16[128,1024]{1,0:T(8,128)(2,1)S(1)} custom-call(f32[8,128]{1,0:T(8,128)} %bitcast.5, f32[1,8]{1,0:T(1,128)} %bitcast.7, f32[1,8]{1,0:T(1,128)} %bitcast.8, f32[1,8]{1,0:T(1,128)} %bitcast.9, f32[1,1024]{1,0:T(1,128)} %bitcast.6, bf16[128,128]{1,0:T(8,128)(2,1)} %b_hbm.1, bf16[128,128]{1,0:T(8,128)(2,1)} %c_hbm.1, bf16[128,1024]{1,0:T(8,128)(2,1)} %x_hbm.1, ...), custom_call_target="tpu_custom_call" | custom-call | tf_op jit(solution)/shard_map/mixer/pallas_call | solution.py:451
  62.9 0.7 %copy.12 = bf16[128,1024]{1,0:T(8,128)(2,1)} copy(bf16[128,1024]{1,0:T(8,128)(2,1)S(1)} %mixer.1) | data formatting | bytes 524288

commit v7 on v6

--- a/solution.py
+++ b/solution.py
@@ -30,7 +30,7 @@
     lsend, lrecv, tsend, trecv,
     rsend, rrecv, dsend, drecv,
     esend, erecv, ssend, srecv,
-    part_sums, precv, xsend, xrecv, fsend,
+    part_sums, precv, xsend, xown, xrecv, fsend,
     in_sems, w_local, w_ss, w_rs, l_ss, l_rs, t_ss, t_rs, r_ss, r_rs, d_ss, d_rs,
     e_ss, e_rs, s_ss, s_rs, a_ss, a_rs, p_ss, p_rs, x_ss, x_rs, f_ss, o_ss, f_rs,
 ):
@@ -300,7 +300,14 @@
         arrived(dst, rs)
         lanes = lanes_of(half)
         both = part_sums[core, n, span[0] : span[1], :, lanes]
-        both = (both + precv[n, span[0] : span[1], :, lanes]).astype(BF16)
+        both = both + precv[n, span[0] : span[1], :, lanes]
+        for j in range(NX):
+
+            @pl.when(x == j)
+            def _():
+                xown[n, span[0] : span[1], :, lanes] = both[:, j * slab : (j + 1) * slab, :]
+
+        both = both.astype(BF16)
         for j in range(NX):
             xsend[n, j, span[0] : span[1], :, lanes] = both[:, j * slab : (j + 1) * slab, :]
         rows = pl.ds(span[0], span[1] - span[0])
@@ -317,7 +324,7 @@
     place = pl.ds(pl.multiple_of(core * share + x * slab, slab), slab)
 
     def finish(n):
-        value = xsend[n, x].astype(F32)
+        value = xown[n]
         arrived(xrecv.at[n], x_rs.at[n])
         for k in range(1, NX):
             value = value + xrecv[n, k - 1].astype(F32)
@@ -434,6 +441,7 @@
         pltpu.VMEM((NC, NZ, NY, share, cols), F32),
         pltpu.VMEM((NZ, NY, share, cols), F32),
         pltpu.VMEM((NZ, NX, NY, share // NX, cols), BF16),
+        pltpu.VMEM((NZ, NY, share // NX, cols), F32),
         pltpu.VMEM((NZ, NX - 1, NY, share // NX, cols), BF16),
         pltpu.VMEM((NZ, NY, share // NX, cols), BF16),
         dma((9,)),

time: 64.6 us -> 64.7 us (level)
  no operation moved by 1% of the time
where the time goes in v7:
time: 64.7 us; the launch traced here: 63.6 us
  Pallas kernels  62.9 us (97%)
  local copies, waits for them, and re-layouts  0.71 us (1%)
    pallas_call x1, Pallas kernels, shards(): pl.pallas_call(kernel, out_shape=pltpu.VMEM((tokens, channels), BF16), in...  62.9 us

profile of v7, /device:TPU:4, one launch (start us, length us, event | category | flops | bytes accessed | tf_op | source)
XLA Modules:
  0.0 63.6 jit_solution(10590175532341959478)
XLA Ops:
  0.0 62.9 %mixer.1 = bf16[128,1024]{1,0:T(8,128)(2,1)S(1)} custom-call(f32[8,128]{1,0:T(8,128)} %bitcast.5, f32[1,8]{1,0:T(1,128)} %bitcast.7, f32[1,8]{1,0:T(1,128)} %bitcast.8, f32[1,8]{1,0:T(1,128)} %bitcast.9, f32[1,1024]{1,0:T(1,128)} %bitcast.6, bf16[128,128]{1,0:T(8,128)(2,1)} %b_hbm.1, bf16[128,128]{1,0:T(8,128)(2,1)} %c_hbm.1, bf16[128,1024]{1,0:T(8,128)(2,1)} %x_hbm.1, ...), custom_call_target="tpu_custom_call" | custom-call | tf_op jit(solution)/shard_map/mixer/pallas_call | solution.py:459
  62.9 0.7 %copy.12 = bf16[128,1024]{1,0:T(8,128)(2,1)} copy(bf16[128,1024]{1,0:T(8,128)(2,1)S(1)} %mixer.1) | data formatting | bytes 524288

commit v8 on v7

--- a/solution.py
+++ b/solution.py
@@ -110,6 +110,9 @@
     items = [(step, i) for step in range(last) for i in range(4)] + [(last, 0), (last, 2)]
     done = [0]
 
+    def place_of(step, i):
+        return 4 * step + (i if step < last - 1 else i // 2)
+
     def relay(count):
         while done[0] < count:
             step, i = items[done[0]]
@@ -122,9 +125,9 @@
                         pl.ds(half * khalf, khalf), pl.ds(i // 2 * chalf, chalf)
                     ]
                 else:
-                    arrived(part, w_rs.at[d, step - 1, i])
+                    arrived(part, w_rs.at[d, place_of(step - 1, i)])
                 if step < last - 1 or (step == last - 1 and i % 2 == 0):
-                    send(source, part, w_ss, w_rs.at[d, step, i], device(dz=sign))
+                    send(source, part, w_ss, w_rs.at[d, place_of(step, i)], device(dz=sign))
 
     relay(3)
 
@@ -158,6 +161,13 @@
             ],
             axis=1,
         )
+    for k in range(1, NY):
+        to = (y + k) % NY
+        send(lsend.at[to], lrecv.at[y], l_ss, l_rs, device(dy=k))
+        send(tsend.at[to, pl.ds(0, 1), :], trecv.at[y, pl.ds(0, 1), :], t_ss, t_rs, device(dy=k))
+    lrecv[y] = lsend[y]
+    trecv[y] = tsend[y]
+
     logits = dot(cmat, bmat, ((1,), (1,)))
     cum_t = jnp.transpose(cum)
     dt_t = jnp.transpose(dt)
@@ -169,13 +179,6 @@
         ybuf[:, span] = dot(high, xh) + dot(low, xh) + skip_ref[:, h : h + 1] * xh.astype(F32)
         gate = m_ref[:, span].astype(F32)
         smbuf[:, span] = gate / (1.0 + jnp.exp(-gate))
-
-    for k in range(1, NY):
-        to = (y + k) % NY
-        send(lsend.at[to], lrecv.at[y], l_ss, l_rs, device(dy=k))
-        send(tsend.at[to, pl.ds(0, 1), :], trecv.at[y, pl.ds(0, 1), :], t_ss, t_rs, device(dy=k))
-    lrecv[y] = lsend[y]
-    trecv[y] = tsend[y]
 
     arrived(lrecv.at[pl.ds(0, NY - 1)], l_rs)
     arrived(trecv.at[pl.ds(0, NY - 1), pl.ds(0, 1), :], t_rs)
@@ -273,7 +276,7 @@
             part_sums.at[1 - core, n, rows, :, lanes_of(half)],
             precv.at[n, rows, :, lanes_of(half)],
             p_ss,
-            p_rs.at[n, index],
+            p_rs.at[3 * n + index if n < 5 else 10 + n + index],
         )
 
     def multiply(n, span, half):
@@ -446,13 +449,13 @@
         pltpu.VMEM((NZ, NY, share // NX, cols), BF16),
         dma((9,)),
         dma((2,)),
-        dma, dma((2, 4, 4)),
+        dma, dma((2, 14)),
         dma, dma, dma, dma,
         dma, dma, dma, dma,
         dma, dma,
         dma, dma,
         dma, dma((2, 3)),
-        dma, dma((NZ, 3)),
+        dma, dma((19,)),
         dma, dma((NZ,)),
         dma, dma, dma,
     ]

time: 64.7 us -> 64.6 us (level)
  no operation moved by 1% of the time
where the time goes in v8:
time: 64.6 us; the launch traced here: 63.5 us
  Pallas kernels  62.8 us (97%)
  local copies, waits for them, and re-layouts  0.71 us (1%)
    pallas_call x1, Pallas kernels, shards(): pl.pallas_call(kernel, out_shape=pltpu.VMEM((tokens, channels), BF16), in...  62.8 us

profile of v8, /device:TPU:4, one launch (start us, length us, event | category | flops | bytes accessed | tf_op | source)
XLA Modules:
  0.0 63.5 jit_solution(3133325751569351037)
XLA Ops:
  0.0 62.8 %mixer.1 = bf16[128,1024]{1,0:T(8,128)(2,1)S(1)} custom-call(f32[8,128]{1,0:T(8,128)} %bitcast.5, f32[1,8]{1,0:T(1,128)} %bitcast.7, f32[1,8]{1,0:T(1,128)} %bitcast.8, f32[1,8]{1,0:T(1,128)} %bitcast.9, f32[1,1024]{1,0:T(1,128)} %bitcast.6, bf16[128,128]{1,0:T(8,128)(2,1)} %b_hbm.1, bf16[128,128]{1,0:T(8,128)(2,1)} %c_hbm.1, bf16[128,1024]{1,0:T(8,128)(2,1)} %x_hbm.1, ...), custom_call_target="tpu_custom_call" | custom-call | tf_op jit(solution)/shard_map/mixer/pallas_call | solution.py:462
  62.8 0.7 %copy.12 = bf16[128,1024]{1,0:T(8,128)(2,1)} copy(bf16[128,1024]{1,0:T(8,128)(2,1)S(1)} %mixer.1) | data formatting | bytes 524288

commit v9 on v8

--- a/solution.py
+++ b/solution.py
@@ -193,7 +193,7 @@
     for k in range(NZ):
         rsend[k] = current[k * size : (k + 1) * size, :].astype(BF16)
     dsend[...] = jnp.broadcast_to(before[NY], (8, pair))
-    for k in range(1, NZ):
+    for k in (4, 3, 5, 2, 6, 1, 7):
         to = (z + k) % NZ
         send(rsend.at[to], rrecv.at[z], r_ss, r_rs, device(dz=k))
         send(dsend.at[pl.ds(0, 1), :], drecv.at[z, pl.ds(0, 1), :], d_ss, d_rs, device(dz=k))
@@ -207,7 +207,7 @@
     for k in range(NZ):
         esend[k] = current.astype(BF16)
         current = jnp.exp(drecv[k][0:1, :]) * current + rrecv[k].astype(F32)
-    for k in range(1, NZ):
+    for k in (4, 3, 5, 2, 6, 1, 7):
         to = (z + k) % NZ
         send(esend.at[to], erecv.at[z], e_ss, e_rs, device(dz=k))
     erecv[z] = esend[z]
@@ -314,7 +314,7 @@
         for j in range(NX):
             xsend[n, j, span[0] : span[1], :, lanes] = both[:, j * slab : (j + 1) * slab, :]
         rows = pl.ds(span[0], span[1] - span[0])
-        for k in range(1, NX):
+        for k in (2, 1, 3):
             send(
                 xsend.at[n, (x + k) % NX, rows, :, lanes],
                 xrecv.at[n, k - 1, rows, :, lanes],

time: 64.6 us -> 64.6 us (level)
  no operation moved by 1% of the time
where the time goes in v9:
time: 64.6 us; the launch traced here: 63.5 us
  Pallas kernels  62.8 us (97%)
  local copies, waits for them, and re-layouts  0.71 us (1%)
    pallas_call x1, Pallas kernels, shards(): pl.pallas_call(kernel, out_shape=pltpu.VMEM((tokens, channels), BF16), in...  62.8 us

profile of v9, /device:TPU:4, one launch (start us, length us, event | category | flops | bytes accessed | tf_op | source)
XLA Modules:
  0.0 63.5 jit_solution(9137156237940893072)
XLA Ops:
  0.0 62.8 %mixer.1 = bf16[128,1024]{1,0:T(8,128)(2,1)S(1)} custom-call(f32[8,128]{1,0:T(8,128)} %bitcast.5, f32[1,8]{1,0:T(1,128)} %bitcast.7, f32[1,8]{1,0:T(1,128)} %bitcast.8, f32[1,8]{1,0:T(1,128)} %bitcast.9, f32[1,1024]{1,0:T(1,128)} %bitcast.6, bf16[128,128]{1,0:T(8,128)(2,1)} %b_hbm.1, bf16[128,128]{1,0:T(8,128)(2,1)} %c_hbm.1, bf16[128,1024]{1,0:T(8,128)(2,1)} %x_hbm.1, ...), custom_call_target="tpu_custom_call" | custom-call | tf_op jit(solution)/shard_map/mixer/pallas_call | solution.py:462
  62.8 0.7 %copy.12 = bf16[128,1024]{1,0:T(8,128)(2,1)} copy(bf16[128,1024]{1,0:T(8,128)(2,1)S(1)} %mixer.1) | data formatting | bytes 524288
